TPU v7x, 256 devices: a whole 4x4x8 slice. The times are simulated.
256 devices in a mesh: row: 8 (over x, y_lo), col: 32 (over y_hi, z, core).
Axes of the slice: x: 4, y: 4 (y_hi: 2, y_lo: 2; y = y_hi * 2 + y_lo), z: 8, core: 2. Of those that a mesh axis runs over, the one named last changes fastest.
Arguments:
- factor: float32 [16384, 16384], P('row', 'col'), may hold values from -7 to 12
Outputs:
- factor_next: float32 [16384, 16384], P('row', 'col')
All inputs are finite; a program needn't handle non-finite values.
Results may differ from a plain program's by a relative error of at most 0.0078.
Values may be sent and summed in bfloat16 or wider, within the bound.
No kernel may reach another device: no remote copies, remote signals or barrier semaphores. Data moves between devices by JAX's collectives and lax.ppermute only.
A program may use at most 64 MiB of HBM per device.

v0:
```python
import math

import jax
import jax.numpy as jnp
import numpy as np
from jax import lax
from jax.experimental import pallas as pl
from jax.experimental.pallas import tpu as pltpu
from jax.sharding import Mesh
from jax.sharding import PartitionSpec as P

N = 512
H = 256
Q = 128
ROWS = 8
COLS = 32
GROUP = 4
ROW = ("x", "yl")
COL = ("yh", "z", "core")
ALL = ROW + COL
BF = jnp.bfloat16
F32 = jnp.float32


def dev(r, c):
    return r * COLS + c


def row_of(x, yl):
    return 2 * x + yl


def col_of(yh, z, core):
    return 16 * yh + 2 * z + core


def move(value, pairs):
    return lax.ppermute(value, ALL, pairs)


GRID = [(r, c) for r in range(ROWS) for c in range(COLS)]


def col_offset(r, c):
    return (r // 2 - c // 8) % 4, (r % 2) ^ ((c // 4) % 2)


def row_offset(r, c):
    return ((c // 2) % 8 - 2 * (r % 4)) % 8, (c // 16) ^ (r // 4)


def flag_table():
    table = np.zeros((ROWS * COLS, 16), np.int32)
    for r, c in GRID:
        local = c - GROUP * r
        dx, dy = col_offset(r, c)
        dz, dyh = row_offset(r, c)
        table[dev(r, c), :12] = [
            min(max(local, 0), GROUP - 1),
            int(0 <= local < GROUP),
            int(c == 0),
            int(c == COLS - 1),
            int(r == 0),
            int(r == ROWS - 1),
            max(c - 2, 0) % GROUP,
            dz,
            c % 2,
            dx,
            dy,
            dyh,
        ]
    return table


def x_pairs(starts, step):
    pairs = []
    for r, c in GRID:
        dx, _ = col_offset(r, c)
        if dx in starts:
            x = (r // 2 + step) % 4
            pairs.append((dev(r, c), dev(row_of(x, r % 2), c)))
    return pairs


YL_FROM_SOURCE = [(dev(k // 4, k), dev((k // 4) ^ 1, k)) for k in range(COLS)]
YL_SWAP = [(dev(r, c), dev(r ^ 1, c)) for r, c in GRID]
CORE_SWAP = [(dev(r, c), dev(r, c ^ 1)) for r, c in GRID]


def z_pairs(step, starts=None, planes=(0, 1)):
    pairs = []
    for r, c in GRID:
        dz, dyh = row_offset(r, c)
        if (starts is None or dz in starts) and dyh in planes:
            z = ((c // 2) % 8 + step) % 8
            pairs.append((dev(r, c), dev(r, col_of(c // 16, z, c % 2))))
    return pairs


SPREAD_TWO = z_pairs(-2, (0,), (0,)) + z_pairs(2, (1,), (0,))
SPREAD_ONE = z_pairs(-1, (0, 6), (0,)) + z_pairs(1, (1, 3), (0,))
YH_COPY = [(dev(r, c), dev(r, c ^ 16)) for r, c in GRID if row_offset(r, c)[1] == 0]
NEXT_DIAG = [(dev(k // 4, k), dev((k + 1) // 4, k + 1)) for k in range(COLS - 1)]
PREV_DIAG = [(dev(k // 4, k), dev((k - 1) // 4, k - 1)) for k in range(1, COLS)]
CROSS = [(dev(max(k - 1, 0) // 4, k + 1), dev(k // 4, k)) for k in range(COLS - 1)]
COL_RIGHT = [(dev(r, c), dev(r, c + 1)) for r, c in GRID if c + 1 < COLS]
COL_LEFT = [(dev(r, c), dev(r, c - 1)) for r, c in GRID if c > 0]
ROW_DOWN = [(dev(r, c), dev(r + 1, c)) for r, c in GRID if r + 1 < ROWS]
ROW_UP = [(dev(r, c), dev(r - 1, c)) for r, c in GRID if r > 0]


def mm(a, b):
    return jnp.dot(a, b, preferred_element_type=F32)


def mm_t(a, b):
    return lax.dot_general(a, b, (((0,), (0,)), ((), ())), preferred_element_type=F32)


def pair_solve(block):
    size = block.shape[0]
    step_size = 0.5 / math.sqrt(size)
    col = lax.broadcasted_iota(jnp.int32, (size, size), 1)
    row = lax.broadcasted_iota(jnp.int32, (size, size), 0)
    scale = (col - row).astype(F32) * (step_size / size)

    def small_part(current):
        skew = current * scale
        narrow = skew.astype(BF)
        excess = skew + skew.T + mm_t(narrow, narrow)
        return skew - 0.5 * (excess + mm(narrow, excess.astype(BF)))

    first = small_part(block)
    first_b = first.astype(BF)
    half_way = block + mm(block.astype(BF), first_b)
    current = half_way + mm_t(first_b, half_way.astype(BF))
    second = small_part(current)
    both = first + second + mm(first_b, second.astype(BF))
    return (both + (col == row).astype(F32)).astype(BF)


def store_rotation(rot, near_ref, far_ref, near_t_ref, far_t_ref):
    turned = rot.T
    for p in range(2):
        near_ref[p] = rot[p * Q : (p + 1) * Q]
        far_ref[p] = rot[H + p * Q : H + (p + 1) * Q]
        near_t_ref[p] = turned[p * Q : (p + 1) * Q]
        far_t_ref[p] = turned[H + p * Q : H + (p + 1) * Q]


def solve_one_body(
    flags, matrix_ref, near, far, near_t, far_t, right_ref, left_ref, hold, sem
):
    @pl.when(flags[1] == 1)
    def _():
        fetched(matrix_ref, flags[0], hold, sem)
        block = hold[...]
        rot = pair_solve(block)
        store_rotation(rot, near, far, near_t, far_t)
        part = mm(block.astype(BF), rot).astype(BF)
        turned = mm_t(rot, part).astype(BF)
        first = flags[2] == 1
        up = jnp.concatenate([rot[:, :H], turned[:H, :H]], 0)
        low = jnp.concatenate([rot[:, H:], turned[H:, H:]], 0)
        right_ref[...] = jnp.where(first, low, up)
        left_ref[...] = jnp.where(first, up, low)


def solve_two_body(
    flags, own_right, own_left, came_right, came_left, cross_ref, last_ref, *outs
):
    @pl.when(flags[1] == 1)
    def _():
        last = flags[3] == 1
        up = jnp.where(flags[2] == 1, own_left[...], came_right[...])
        low = jnp.where(last, own_right[...], came_left[...])
        cross = jnp.where(last, last_ref[...], cross_ref[...])
        mixed = mm_t(up[:N], mm(cross, low[:N]).astype(BF))
        block = jnp.concatenate(
            [
                jnp.concatenate([up[N:].astype(F32), mixed], 1),
                jnp.concatenate([mixed.T, low[N:].astype(F32)], 1),
            ],
            0,
        )
        store_rotation(pair_solve(block), *outs)


def whole(shape):
    return pl.BlockSpec(shape, lambda i, f: (0,) * len(shape))


ANYWHERE = pl.BlockSpec(memory_space=pl.ANY)
IN_HBM = pl.BlockSpec(memory_space=pltpu.MemorySpace.HBM)
FETCH = [pltpu.VMEM((N, N), F32), pltpu.SemaphoreType.DMA]


def call(body, flags, args, in_specs, out_specs, out_shape, grid, scratch=(), **kw):
    return pl.pallas_call(
        body,
        grid_spec=pltpu.PrefetchScalarGridSpec(
            num_scalar_prefetch=1,
            grid=grid,
            in_specs=in_specs,
            out_specs=out_specs,
            scratch_shapes=scratch,
        ),
        out_shape=out_shape,
        compiler_params=pltpu.CompilerParams(dimension_semantics=("arbitrary",), vmem_limit_bytes=24 << 20
        ),
        **kw,
    )(flags, *args)


def shape(*dims, dtype=BF):
    return jax.ShapeDtypeStruct(dims, dtype)


def solve_one(flags, matrix):
    return call(
        solve_one_body,
        flags,
        (matrix,),
        [IN_HBM],
        [whole((2, Q, N))] * 4 + [whole((N + H, H))] * 2,
        [shape(2, Q, N)] * 4 + [shape(N + H, H)] * 2,
        (1,),
        scratch=FETCH,
        name="solve_one",
    )


def solve_two(flags, right, left, came_right, came_left, cross, last):
    message = whole((N + H, H))
    return call(
        solve_two_body,
        flags,
        (right, left, came_right, came_left, cross, last),
        [message] * 4 + [whole((N, N))] * 2,
        [whole((2, Q, N))] * 4,
        [shape(2, Q, N)] * 4,
        (1,),
        name="solve_two",
    )


def fetched(matrix_ref, slot, hold, sem):
    copy = pltpu.make_async_copy(matrix_ref.at[pl.ds(slot * N, N), :], hold, sem)
    copy.start()
    copy.wait()


def cast_body(flags, matrix_ref, out_ref, last_ref, hold, sem):
    fetched(matrix_ref, flags[6], hold, sem)
    out_ref[...] = hold[...].astype(BF)

    @pl.when(flags[3] == 1)
    def _():
        fetched(matrix_ref, GROUP - 2, hold, sem)
        last_ref[...] = hold[...].astype(BF)


def cross_block(flags, matrix):
    return call(
        cast_body,
        flags,
        (matrix,),
        [IN_HBM],
        [whole((N, N))] * 2,
        [shape(N, N)] * 2,
        (1,),
        scratch=FETCH,
        name="cross_block",
    )


EDGE = (0, 3)
INNER = (1, 1)


def store_halves(flags, product, right_ref, left_ref):
    up = product[:, :H]
    low = product[:, H:]
    first = flags[2] == 1
    right_ref[...] = jnp.where(first, low, up)
    left_ref[...] = jnp.where(first, up, low)


def joined(flags, own_right, own_left, came_right, came_left):
    up = jnp.where(flags[2] == 1, own_left[...], came_right[...])
    low = jnp.where(flags[3] == 1, own_right[...], came_left[...])
    return jnp.concatenate([up, low], 1)


def half_specs(base, stride):
    return [
        pl.BlockSpec((N, H), lambda i, f: ((base + stride * i) * f[3], 0)),
        pl.BlockSpec((N, H), lambda i, f: ((base + stride * i) * f[2], 0)),
        pl.BlockSpec((N, H), lambda i, f: (base + stride * i, 0)),
        pl.BlockSpec((N, H), lambda i, f: (base + stride * i, 0)),
    ]


def right_one_body(flags, block_ref, rot_ref, right_ref, left_ref):
    product = mm(block_ref[...].astype(BF), rot_ref[...].reshape(N, N)).astype(BF)
    store_halves(flags, product, right_ref, left_ref)


def right_two_body(flags, *refs):
    rot_ref, right_ref, left_ref = refs[4:]
    product = mm(joined(flags, *refs[:4]), rot_ref[...].reshape(N, N)).astype(BF)
    store_halves(flags, product, right_ref, left_ref)


def right(flags, sources, rot, slot):
    out = pl.BlockSpec((N, H), lambda i, f: (i, 0))
    first = slot == 0
    return call(
        right_one_body if first else right_two_body,
        flags,
        (*sources, rot),
        ([pl.BlockSpec((N, N), lambda i, f: (i, 0))] if first else half_specs(0, 1))
        + [pl.BlockSpec((4, 1, Q, N), lambda i, f: (0, slot, 0, 0))],
        [out, out],
        [shape(GROUP * N, H)] * 2,
        (GROUP,),
        name="right",
    )


def row_rotation(flags, i, mine, theirs):
    own_line = (i % 2) == flags[8]
    lower = i // 2
    parts = []
    for p in range(4):
        owner = jnp.where(lower == 1, 1 + p, (8 - p) % 8)
        spot = lax.rem(owner + 8 - flags[7], 8)
        parts.append(jnp.where(own_line, mine[spot, 0], theirs[spot, 0]))
    return jnp.concatenate(parts, 0)


def with_ends(flags, step, main_ref, above_ref, below_ref):
    block = main_ref[...]
    take_above = jnp.logical_and(step == 0, flags[4] == 0)
    take_below = jnp.logical_and(step == 1, flags[5] == 0)
    above = jnp.where(take_above, above_ref[...], block[:H])
    below = jnp.where(take_below, below_ref[...], block[H:])
    return jnp.concatenate([above, below], 0)


def left_body(pairs, slot, flags, *refs):
    base, stride = pairs
    step = pl.program_id(0)
    edge = pairs == EDGE
    mine, theirs = refs[:2]
    if slot == 0:
        block = joined(flags, *refs[2:6])
        rest = refs[6:]
    elif edge:
        block = with_ends(flags, step, *refs[2:5])
        rest = refs[5:]
    else:
        block = refs[2][...]
        rest = refs[3:]
    if edge:
        out_ref, down_ref, up_ref, hold, sems = rest
    else:
        out_ref, hold, sems = rest[1:]
    i = base + stride * step
    product = mm(row_rotation(flags, i, mine, theirs), block)
    up = product[:H].astype(hold.dtype)
    low = product[H:].astype(hold.dtype)
    hold[2 * step] = up
    hold[2 * step + 1] = low
    if edge:
        top = flags[4]
        up_spot = jnp.where(step == 0, 2 - 2 * top, 7)
        low_spot = jnp.where(step == 0, 2 * top, 5)

        @pl.when(step == 0)
        def _():
            up_ref[...] = low.astype(BF)

        @pl.when(step == 1)
        def _():
            down_ref[...] = up.astype(BF)
    else:
        up_spot = 2 * i + 2
        low_spot = 2 * i - 1

    def copies(s, up_at, low_at):
        return (
            pltpu.make_async_copy(
                hold.at[2 * s], out_ref.at[pl.ds(up_at * H, H), :], sems.at[2 * s]
            ),
            pltpu.make_async_copy(
                hold.at[2 * s + 1], out_ref.at[pl.ds(low_at * H, H), :], sems.at[2 * s + 1]
            ),
        )

    for copy in copies(step, up_spot, low_spot):
        copy.start()

    @pl.when(step == 1)
    def _():
        for s in range(2):
            for copy in copies(s, s, s):
                copy.wait()


def left(flags, rows, slot, pairs, sources, ends=(), target=None):
    base, stride = pairs
    edge = pairs == EDGE
    pieces = pl.BlockSpec((8, 1, Q, N), lambda i, f: (0, slot, 0, 0))
    if slot == 0:
        specs = half_specs(base, stride)
    else:
        specs = [pl.BlockSpec((N, N), lambda i, f: (base + stride * i, 0))]
    specs = specs + [whole((H, N))] * len(ends)
    dtype = BF if slot == 0 else F32
    args = (*rows, *sources, *ends)
    return call(
        lambda *refs: left_body(pairs, slot, *refs),
        flags,
        args if edge else (*args, target),
        [pieces, pieces, *specs] + ([] if edge else [ANYWHERE]),
        [ANYWHERE] + ([whole((H, N))] * 2 if edge else []),
        [shape(GROUP * N, N, dtype=dtype)] + ([shape(H, N)] * 2 if edge else []),
        (2,),
        scratch=[pltpu.VMEM((4, H, N), dtype), pltpu.SemaphoreType.DMA((4,))],
        input_output_aliases={} if edge else {len(args) + 1: 0},
        name="left_edge" if edge else "left_inner",
    )


def settle_body(flags, above_ref, below_ref, main_ref, out_ref, hold, sems):
    first = pltpu.make_async_copy(hold.at[0], out_ref.at[pl.ds(0, H), :], sems.at[0])
    last = pltpu.make_async_copy(
        hold.at[1], out_ref.at[pl.ds((2 * GROUP - 1) * H, H), :], sems.at[1]
    )

    @pl.when(flags[4] == 0)
    def _():
        hold[0] = above_ref[...].astype(F32)
        first.start()

    @pl.when(flags[5] == 0)
    def _():
        hold[1] = below_ref[...].astype(F32)
        last.start()

    @pl.when(flags[4] == 0)
    def _():
        first.wait()

    @pl.when(flags[5] == 0)
    def _():
        last.wait()


def settle(flags, main, above, below):
    return call(
        settle_body,
        flags,
        (above, below, main),
        [whole((H, N)), whole((H, N)), ANYWHERE],
        ANYWHERE,
        shape(GROUP * N, N, dtype=F32),
        (1,),
        scratch=[pltpu.VMEM((2, H, N), F32), pltpu.SemaphoreType.DMA((2,))],
        input_output_aliases={3: 0},
        name="settle",
    )


def exchange_columns(halves):
    return (*halves, move(halves[0], COL_RIGHT), move(halves[1], COL_LEFT))


def steps(factor):
    x = lax.axis_index("x")
    yl = lax.axis_index("yl")
    yh = lax.axis_index("yh")
    z = lax.axis_index("z")
    core = lax.axis_index("core")
    r = 2 * x + yl
    c = 16 * yh + 2 * z + core
    dx = (x - c // 8) & 3
    dy = yl ^ ((c // 4) & 1)
    dz = (z - 2 * (r & 3)) & 7
    dyh = yh ^ (r // 4)
    flags = lax.dynamic_index_in_dim(
        jnp.asarray(flag_table()), r * COLS + c, 0, keepdims=False
    )

    cross_out, cross_last = cross_block(flags, factor)
    cross = move(cross_out, CROSS)
    *rot_one, to_right, to_left = solve_one(flags, factor)
    from_left = move(to_right, NEXT_DIAG)
    from_right = move(to_left, PREV_DIAG)

    def out_of_source(rot):
        near, far, near_t, far_t = rot
        held = jnp.where(dz < 2, near_t, move(far_t, SPREAD_TWO))
        start = jnp.where(dy == 0, near, move(far, YL_FROM_SOURCE))
        return start, held

    sent_one = out_of_source(rot_one)
    rot_two = solve_two(flags, to_right, to_left, from_left, from_right, cross, cross_last)
    sent_two = out_of_source(rot_two)
    start = jnp.stack([sent_one[0], sent_two[0]], 1)
    held = jnp.stack([sent_one[1], sent_two[1]], 1)

    nearer = move(held[1], SPREAD_ONE)
    fore = move(start[0], x_pairs((0,), 1))
    back = move(start[1], x_pairs((0,), -1))
    fore_message = jnp.where(dx == 0, start[1], fore)
    back_message = jnp.where(dx == 0, start[0], back)
    take = (dz == 7) | (dz == 2) | (dz == 5) | (dz == 4)
    piece = jnp.where(take, nearer, held[0])

    copied = move(piece, YH_COPY)
    fore_next = move(fore_message, x_pairs((0, 1), 1))
    back_next = move(back_message, x_pairs((0, 3), -1))
    low = jnp.where(
        dx == 0, start[0], jnp.where(dx == 1, fore, jnp.where(dx == 2, fore_next, back_next))
    )
    high = jnp.where(
        dx == 0, start[1], jnp.where(dx == 1, fore_next, jnp.where(dx == 2, back_next, back))
    )
    mine = jnp.stack([low, high])
    piece = jnp.where(dyh == 0, piece, copied)

    other = move(mine, YL_SWAP)
    ahead = [piece]
    behind = [piece]

    def ring():
        ahead.append(move(ahead[-1], z_pairs(1)))
        behind.append(move(behind[-1], z_pairs(-1)))

    ring()
    ring()
    cols = jnp.concatenate(
        [jnp.where(dy == 0, mine, other), jnp.where(dy == 0, other, mine)], 0
    )
    halves = right(flags, (factor,), cols, 0)
    ring()
    halves = exchange_columns(halves)
    last = (move(ahead[3][0], z_pairs(1)), move(behind[3][1], z_pairs(-1)))
    halves = right(flags, halves, cols, 1)
    halves = exchange_columns(halves)
    line = jnp.stack(
        [piece, *behind[1:], jnp.stack(last), ahead[3], ahead[2], ahead[1]]
    )
    rows = line, move(line, CORE_SWAP)

    main, down, up = left(flags, rows, 0, EDGE, halves)
    above = move(down, ROW_DOWN)
    below = move(up, ROW_UP)
    (main,) = left(flags, rows, 0, INNER, halves, target=main)
    out, down, up = left(flags, rows, 1, EDGE, (main,), (above, below))
    last_above = move(down, ROW_DOWN)
    last_below = move(up, ROW_UP)
    (out,) = left(flags, rows, 1, INNER, (main,), target=out)
    return settle(flags, out, last_above, last_below)


def solution(mesh):
    split = Mesh(mesh.devices.reshape(4, 2, 2, 8, 2), ALL)
    placed = P(ROW, COL)
    return jax.shard_map(
        steps, mesh=split, in_specs=(placed,), out_specs=placed, check_vma=False
    )
```

profile of v0, /device:TPU:26, one launch (start us, length us, event | category | flops | bytes accessed | tf_op | source)
XLA Modules:
  0.0 175.6 jit_solution(5432634823844102491)
XLA Ops:
  0.7 2.2 %copy-done = f32[2048,512]{1,0:T(8,128)S(1)} copy-done((f32[2048,512]{1,0:T(8,128)S(1)}, f32[2048,512]{1,0:T(8,128)}, u32[]{:S(2)}) %copy-start) | copy-done | bytes 4194328
  2.9 1.5 cross_block.1
  4.4 7.9 %collective-permute-start.3 = (bf16[512,512]{1,0:T(8,128)(2,1)}, bf16[512,512]{1,0:T(8,128)(2,1)S(1)}, u32[]{:S(2)}, u32[]{:S(2)}) collective-permute-start(bf16[512,512]{1,0:T(8,128)(2,1)} %get-tuple-element.31), channel_id=1, source_target_pairs={{1,0},{2,1},{3,2},{4,3},{5,36},{38,37},{39,38},{40,39},{41,72},{74... | collective-permute-start | bytes 1572872 | tf_op jit(solution)/shard_map/ppermute | solution.py:38
  12.3 1.3 solve_one.1
  14.9 1.4 collective-permute-start
  16.3 1.4 collective-permute-start.16
  17.7 1.6 collective-permute-done.3.cross_ref
  20.5 1.0 select_bitcast_fusion.5
  21.5 1.0 select_bitcast_fusion.3
  24.0 1.3 collective-permute-start.20
  25.4 1.3 collective-permute-start.6
  26.7 23.1 %collective-permute-done.20 = bf16[2,128,512]{2,1,0:T(8,128)(2,1)S(1)} collective-permute-done((bf16[2,128,512]{2,1,0:T(8,128)(2,1)S(1)}, bf16[2,128,512]{2,1,0:T(8,128)(2,1)S(1)}, u32[]{:S(2)}, u32[]{:S(2)}) %collective-permute-start.20) | collective-permute-done | bytes 262176 | tf_op jit(solution)/shard_map/ppermute | solution.py:38
  51.2 1.9 %collective-permute-start.21 = (bf16[2,128,512]{2,1,0:T(8,128)(2,1)}, bf16[2,128,512]{2,1,0:T(8,128)(2,1)}, u32[]{:S(2)}, u32[]{:S(2)}) collective-permute-start(bf16[2,128,512]{2,1,0:T(8,128)(2,1)} %get-tuple-element.49), channel_id=1, source_target_pairs={{0,192},{1,193},{2,194},{3,195},{4,196},{5,197},{6,198},{7,199},{8... | collective-permute-start | bytes 786440 | tf_op jit(solution)/shard_map/ppermute | solution.py:38
  53.2 1.8 %bitcast_dynamic-update-slice_fusion.6 = (bf16[8,2,128,512]{3,2,1,0:T(8,128)(2,1)S(1)}, bf16[2,128,512]{2,1,0:T(8,128)(2,1)}) fusion(bf16[2,128,512]{2,1,0:T(8,128)(2,1)S(1)} %fusion.6, bf16[2,128,512]{2,1,0:T(8,128)(2,1)} %collective-permute-done.6, pred[]{:T(512)S(6)} %eq.35), kind=kLoop, calls=%fused_computation.25 | loop fusion | flops 131071 | bytes 1048577
  54.9 1.2 collective-permute-start.7
  56.1 0.8 collective-permute-start.10
  56.9 0.7 broadcast_select_fusion.3
  58.4 5.7 %collective-permute-done.7 = bf16[2,128,512]{2,1,0:T(8,128)(2,1)} collective-permute-done((bf16[2,128,512]{2,1,0:T(8,128)(2,1)}, bf16[2,128,512]{2,1,0:T(8,128)(2,1)}, u32[]{:S(2)}, u32[]{:S(2)}) %collective-permute-start.7) | collective-permute-done | bytes 262176 | tf_op jit(solution)/shard_map/ppermute | solution.py:38
  64.0 2.0 %collective-permute-start.8 = (bf16[2,128,512]{2,1,0:T(8,128)(2,1)}, bf16[2,128,512]{2,1,0:T(8,128)(2,1)S(1)}, u32[]{:S(2)}, u32[]{:S(2)}) collective-permute-start(bf16[2,128,512]{2,1,0:T(8,128)(2,1)} %collective-permute-done.7), channel_id=1, source_target_pairs={{0,14},{1,15},{2,0},{3,1},{4,2},{5,3},{6,4},{7,5},{8,6},{9,7},{10,... | collective-permute-start | bytes 786440 | tf_op jit(solution)/shard_map/ppermute | solution.py:38
  66.1 1.0 select_bitcast_fusion.1
  67.2 1.4 collective-permute-start.22
  68.6 4.2 %collective-permute-done.8 = bf16[2,128,512]{2,1,0:T(8,128)(2,1)S(1)} collective-permute-done((bf16[2,128,512]{2,1,0:T(8,128)(2,1)}, bf16[2,128,512]{2,1,0:T(8,128)(2,1)S(1)}, u32[]{:S(2)}, u32[]{:S(2)}) %collective-permute-start.8) | collective-permute-done | bytes 262176 | tf_op jit(solution)/shard_map/ppermute | solution.py:38
  72.8 2.0 %collective-permute-start.9 = (bf16[2,128,512]{2,1,0:T(8,128)(2,1)S(1)}, bf16[2,128,512]{2,1,0:T(8,128)(2,1)S(1)}, u32[]{:S(2)}, u32[]{:S(2)}) collective-permute-start(bf16[2,128,512]{2,1,0:T(8,128)(2,1)S(1)} %collective-permute-done.8), channel_id=1, source_target_pairs={{0,14},{1,15},{2,0},{3,1},{4,2},{5,3},{6,4},{7,5},{8,6},{9,7},{10,... | collective-permute-start | bytes 786440 | tf_op jit(solution)/shard_map/ppermute | solution.py:38
  74.9 1.0 bitcast_dynamic-update-slice_fusion.5
  76.0 4.6 %collective-permute-done.9 = bf16[2,128,512]{2,1,0:T(8,128)(2,1)S(1)} collective-permute-done((bf16[2,128,512]{2,1,0:T(8,128)(2,1)S(1)}, bf16[2,128,512]{2,1,0:T(8,128)(2,1)S(1)}, u32[]{:S(2)}, u32[]{:S(2)}) %collective-permute-start.9) | collective-permute-done | bytes 262176 | tf_op jit(solution)/shard_map/ppermute | solution.py:38
  80.6 2.5 %collective-permute-start.14 = (bf16[128,512]{1,0:T(8,128)(2,1)S(1)}, bf16[128,512]{1,0:T(8,128)(2,1)S(1)}, u32[]{:S(2)}, u32[]{:S(2)}) collective-permute-start(bf16[128,512]{1,0:T(8,128)(2,1)S(1)} %slice_bitcast_fusion), channel_id=1, source_target_pairs={{0,14},{1,15},{2,0},{3,1},{4,2},{5,3},{6,4},{7,5},{8,6},{9,7},{10,... | collective-permute-start | bytes 393224 | tf_op jit(solution)/shard_map/ppermute | solution.py:38
  84.1 1.9 %copy-done.1 = f32[2048,512]{1,0:T(8,128)S(1)} copy-done((f32[2048,512]{1,0:T(8,128)S(1)}, f32[2048,512]{1,0:T(8,128)}, u32[]{:S(2)}) %copy-start.1) | copy-done | bytes 4194328
  86.0 2.4 %right.2 = (bf16[2048,256]{1,0:T(8,128)(2,1)S(1)}, bf16[2048,256]{1,0:T(8,128)(2,1)S(1)}) custom-call(s32[16]{0:T(128)S(1)} %dynamic-slice_bitcast_fusion.flags.refs_0_, f32[2048,512]{1,0:T(8,128)S(1)} %copy-done.1, bf16[4,2,128,512]{3,2,1,0:T(8,128)(2,1)S(1)} %pad_maximum_fusion.rot_ref.refs_4_), custom_call_target="tpu_custom_call" | custom-call | tf_op jit(solution)/shard_map/right/pallas_call | solution.py:199
  88.4 1.9 %collective-permute-start.23 = (bf16[2048,256]{1,0:T(8,128)(2,1)S(1)}, bf16[2048,256]{1,0:T(8,128)(2,1)S(1)}, u32[]{:S(2)}, u32[]{:S(2)}) collective-permute-start(bf16[2048,256]{1,0:T(8,128)(2,1)S(1)} %get-tuple-element.39.refs_0_), channel_id=1, source_target_pairs={{0,1},{1,2},{2,3},{3,4},{4,5},{5,6},{6,7},{7,8},{8,9},{9,10},{10,1... | collective-permute-start | bytes 3145736 | tf_op jit(solution)/shard_map/ppermute | solution.py:38
  90.3 7.3 %collective-permute-start.24 = (bf16[2048,256]{1,0:T(8,128)(2,1)S(1)}, bf16[2048,256]{1,0:T(8,128)(2,1)S(1)}, u32[]{:S(2)}, u32[]{:S(2)}) collective-permute-start(bf16[2048,256]{1,0:T(8,128)(2,1)S(1)} %get-tuple-element.40.refs_1_), channel_id=1, source_target_pairs={{1,0},{2,1},{3,2},{4,3},{5,4},{6,5},{7,6},{8,7},{9,8},{10,9},{11,1... | collective-permute-start | bytes 3145736 | tf_op jit(solution)/shard_map/ppermute | solution.py:38
  97.7 1.0 bitcast_dynamic-update-slice_fusion.refs_1_
  98.8 9.3 %collective-permute-done.23.refs_2_ = bf16[2048,256]{1,0:T(8,128)(2,1)S(1)} collective-permute-done((bf16[2048,256]{1,0:T(8,128)(2,1)S(1)}, bf16[2048,256]{1,0:T(8,128)(2,1)S(1)}, u32[]{:S(2)}, u32[]{:S(2)}) %collective-permute-start.23) | collective-permute-done | bytes 1048608 | tf_op jit(solution)/shard_map/ppermute | solution.py:38
  108.1 1.8 collective-permute-done.24.refs_3_
  109.9 2.4 %right.3 = (bf16[2048,256]{1,0:T(8,128)(2,1)S(1)}, bf16[2048,256]{1,0:T(8,128)(2,1)S(1)}) custom-call(s32[16]{0:T(128)S(1)} %dynamic-slice_bitcast_fusion.flags.refs_0_, bf16[2048,256]{1,0:T(8,128)(2,1)S(1)} %get-tuple-element.39.refs_0_, bf16[2048,256]{1,0:T(8,128)(2,1)S(1)} %get-tuple-element.40.refs_1_, ...), custom_call_target="tpu_custom_call" | custom-call | tf_op jit(solution)/shard_map/right/pallas_call | solution.py:199
  112.3 1.9 %collective-permute-start.25 = (bf16[2048,256]{1,0:T(8,128)(2,1)S(1)}, bf16[2048,256]{1,0:T(8,128)(2,1)S(1)}, u32[]{:S(2)}, u32[]{:S(2)}) collective-permute-start(bf16[2048,256]{1,0:T(8,128)(2,1)S(1)} %get-tuple-element.41.refs_3_), channel_id=1, source_target_pairs={{0,1},{1,2},{2,3},{3,4},{4,5},{5,6},{6,7},{7,8},{8,9},{9,10},{10,1... | collective-permute-start | bytes 3145736 | tf_op jit(solution)/shard_map/ppermute | solution.py:38
  114.2 7.4 %collective-permute-start.26 = (bf16[2048,256]{1,0:T(8,128)(2,1)S(1)}, bf16[2048,256]{1,0:T(8,128)(2,1)S(1)}, u32[]{:S(2)}, u32[]{:S(2)}) collective-permute-start(bf16[2048,256]{1,0:T(8,128)(2,1)S(1)} %get-tuple-element.42.refs_4_), channel_id=1, source_target_pairs={{1,0},{2,1},{3,2},{4,3},{5,4},{6,5},{7,6},{8,7},{9,8},{10,9},{11,1... | collective-permute-start | bytes 3145736 | tf_op jit(solution)/shard_map/ppermute | solution.py:38
  121.6 13.4 %collective-permute-done.25.refs_5_ = bf16[2048,256]{1,0:T(8,128)(2,1)S(1)} collective-permute-done((bf16[2048,256]{1,0:T(8,128)(2,1)S(1)}, bf16[2048,256]{1,0:T(8,128)(2,1)S(1)}, u32[]{:S(2)}, u32[]{:S(2)}) %collective-permute-start.25) | collective-permute-done | bytes 1048608 | tf_op jit(solution)/shard_map/ppermute | solution.py:38
  135.3 1.8 %left_edge.2 = (bf16[2048,512]{1,0:T(8,128)(2,1)S(1)}, bf16[256,512]{1,0:T(8,128)(2,1)S(1)}, bf16[256,512]{1,0:T(8,128)(2,1)S(1)}) custom-call(s32[16]{0:T(128)S(1)} %dynamic-slice_bitcast_fusion.flags.refs_0_, bf16[8,2,128,512]{3,2,1,0:T(8,128)(2,1)S(1)} %bitcast_dynamic-update-slice_fusion.refs_1_, ...), custom_call_target="tpu_custom_call" | custom-call | tf_op jit(solution)/shard_map/left_edge/pallas_call | solution.py:199
  137.1 7.4 %collective-permute-start.27 = (bf16[256,512]{1,0:T(8,128)(2,1)S(1)}, bf16[256,512]{1,0:T(8,128)(2,1)S(1)}, u32[]{:S(2)}, u32[]{:S(2)}) collective-permute-start(bf16[256,512]{1,0:T(8,128)(2,1)S(1)} %get-tuple-element.44), channel_id=1, source_target_pairs={{0,32},{1,33},{2,34},{3,35},{4,36},{5,37},{6,38},{7,39},{8,40},{9,... | collective-permute-start | bytes 786440 | tf_op jit(solution)/shard_map/ppermute | solution.py:38
  144.6 1.9 %collective-permute-start.28 = (bf16[256,512]{1,0:T(8,128)(2,1)S(1)}, bf16[256,512]{1,0:T(8,128)(2,1)S(1)}, u32[]{:S(2)}, u32[]{:S(2)}) collective-permute-start(bf16[256,512]{1,0:T(8,128)(2,1)S(1)} %get-tuple-element.45), channel_id=1, source_target_pairs={{32,0},{33,1},{34,2},{35,3},{36,4},{37,5},{38,6},{39,7},{40,8},{41... | collective-permute-start | bytes 786440 | tf_op jit(solution)/shard_map/ppermute | solution.py:38
  146.5 1.7 left_inner.2.refs_3_
  148.9 7.3 %collective-permute-done.28.refs_5_ = bf16[256,512]{1,0:T(8,128)(2,1)S(1)} collective-permute-done((bf16[256,512]{1,0:T(8,128)(2,1)S(1)}, bf16[256,512]{1,0:T(8,128)(2,1)S(1)}, u32[]{:S(2)}, u32[]{:S(2)}) %collective-permute-start.28) | collective-permute-done | bytes 262176 | tf_op jit(solution)/shard_map/ppermute | solution.py:38
  156.2 2.7 %left_edge.3 = (f32[2048,512]{1,0:T(8,128)}, bf16[256,512]{1,0:T(8,128)(2,1)S(1)}, bf16[256,512]{1,0:T(8,128)(2,1)S(1)}) custom-call(s32[16]{0:T(128)S(1)} %dynamic-slice_bitcast_fusion.flags.refs_0_, bf16[8,2,128,512]{3,2,1,0:T(8,128)(2,1)S(1)} %bitcast_dynamic-update-slice_fusion.refs_1_, bf16[8,2,128,512]{3,2,1,0:T(8,128)(2,1)S(1)} %collective-permute-done.15.refs_2_, ...), custom_call_target="tpu_custom_call" | custom-call | tf_op jit(solution)/shard_map/left_edge/pallas_call | solution.py:199
  158.9 5.9 %collective-permute-start.29 = (bf16[256,512]{1,0:T(8,128)(2,1)S(1)}, bf16[256,512]{1,0:T(8,128)(2,1)S(1)}, u32[]{:S(2)}, u32[]{:S(2)}) collective-permute-start(bf16[256,512]{1,0:T(8,128)(2,1)S(1)} %get-tuple-element.46), channel_id=1, source_target_pairs={{0,32},{1,33},{2,34},{3,35},{4,36},{5,37},{6,38},{7,39},{8,40},{9,... | collective-permute-start | bytes 786440 | tf_op jit(solution)/shard_map/ppermute | solution.py:38
  164.8 1.9 %collective-permute-start.30 = (bf16[256,512]{1,0:T(8,128)(2,1)S(1)}, bf16[256,512]{1,0:T(8,128)(2,1)S(1)}, u32[]{:S(2)}, u32[]{:S(2)}) collective-permute-start(bf16[256,512]{1,0:T(8,128)(2,1)S(1)} %get-tuple-element.47), channel_id=1, source_target_pairs={{32,0},{33,1},{34,2},{35,3},{36,4},{37,5},{38,6},{39,7},{40,8},{41... | collective-permute-start | bytes 786440 | tf_op jit(solution)/shard_map/ppermute | solution.py:38
  166.7 2.6 %left_inner.3.main_ref = f32[2048,512]{1,0:T(8,128)} custom-call(s32[16]{0:T(128)S(1)} %dynamic-slice_bitcast_fusion.flags.refs_0_, bf16[8,2,128,512]{3,2,1,0:T(8,128)(2,1)S(1)} %bitcast_dynamic-update-slice_fusion.refs_1_, bf16[8,2,128,512]{3,2,1,0:T(8,128)(2,1)S(1)} %collective-permute-done.15.refs_2_, ...), custom_call_target="tpu_custom_call", output_to_operand_aliasing={{}: (4, {})} | custom-call | tf_op jit(solution)/shard_map/left_inner/pallas_call | solution.py:199
  169.3 4.6 %collective-permute-done.30.below_ref = bf16[256,512]{1,0:T(8,128)(2,1)S(1)} collective-permute-done((bf16[256,512]{1,0:T(8,128)(2,1)S(1)}, bf16[256,512]{1,0:T(8,128)(2,1)S(1)}, u32[]{:S(2)}, u32[]{:S(2)}) %collective-permute-start.30) | collective-permute-done | bytes 262176 | tf_op jit(solution)/shard_map/ppermute | solution.py:38
  173.9 1.6 settle.1
  (52 shorter events, 9.1 us)
Async XLA Ops:
  0.7 2.2 %copy-start = (f32[2048,512]{1,0:T(8,128)S(1)}, f32[2048,512]{1,0:T(8,128)}, u32[]{:S(2)}) copy-start(f32[2048,512]{1,0:T(8,128)} %block_ref.1) | copy-start | bytes 12582916
  4.4 14.9 %collective-permute-start.3 = (bf16[512,512]{1,0:T(8,128)(2,1)}, bf16[512,512]{1,0:T(8,128)(2,1)S(1)}, u32[]{:S(2)}, u32[]{:S(2)}) collective-permute-start(bf16[512,512]{1,0:T(8,128)(2,1)} %get-tuple-element.31), channel_id=1, source_target_pairs={{1,0},{2,1},{3,2},{4,3},{5,36},{38,37},{39,38},{40,39},{41,72},{74... | collective-permute-start | bytes 1572872 | tf_op jit(solution)/shard_map/ppermute | solution.py:38
  13.5 4.1 %collective-permute-start.1 = (bf16[768,256]{1,0:T(8,128)(2,1)S(1)}, bf16[768,256]{1,0:T(8,128)(2,1)S(1)}, u32[]{:S(2)}, u32[]{:S(2)}) collective-permute-start(bf16[768,256]{1,0:T(8,128)(2,1)S(1)} %get-tuple-element.29.own_right), channel_id=1, source_target_pairs={{0,1},{1,2},{2,3},{3,36},{36,37},{37,38},{38,39},{39,72},{72,73},{... | collective-permute-start | bytes 1179656 | tf_op jit(solution)/shard_map/ppermute | solution.py:38
  14.2 3.4 %collective-permute-start.2 = (bf16[768,256]{1,0:T(8,128)(2,1)S(1)}, bf16[768,256]{1,0:T(8,128)(2,1)S(1)}, u32[]{:S(2)}, u32[]{:S(2)}) collective-permute-start(bf16[768,256]{1,0:T(8,128)(2,1)S(1)} %get-tuple-element.30.own_left), channel_id=1, source_target_pairs={{1,0},{2,1},{3,2},{36,3},{37,36},{38,37},{39,38},{72,39},{73,72},{... | collective-permute-start | bytes 1179656 | tf_op jit(solution)/shard_map/ppermute | solution.py:38
  14.9 5.6 %collective-permute-start = (bf16[2,128,512]{2,1,0:T(8,128)(2,1)}, bf16[2,128,512]{2,1,0:T(8,128)(2,1)}, u32[]{:S(2)}, u32[]{:S(2)}) collective-permute-start(bf16[2,128,512]{2,1,0:T(8,128)(2,1)} %get-tuple-element.28), channel_id=1, source_target_pairs={{0,12},{1,13},{36,32},{37,33},{72,68},{73,69},{108,104},{109,105},... | collective-permute-start | bytes 786440 | tf_op jit(solution)/shard_map/ppermute | solution.py:38
  16.3 5.2 %collective-permute-start.16 = (bf16[2,128,512]{2,1,0:T(8,128)(2,1)S(1)}, bf16[2,128,512]{2,1,0:T(8,128)(2,1)}, u32[]{:S(2)}, u32[]{:S(2)}) collective-permute-start(bf16[2,128,512]{2,1,0:T(8,128)(2,1)S(1)} %get-tuple-element.36), channel_id=1, source_target_pairs={{0,32},{1,33},{2,34},{3,35},{36,4},{37,5},{38,6},{39,7},{72,104},{... | collective-permute-start | bytes 786440 | tf_op jit(solution)/shard_map/ppermute | solution.py:38
  19.8 3.4 %collective-permute-start.4 = (bf16[2,128,512]{2,1,0:T(8,128)(2,1)S(1)}, bf16[2,128,512]{2,1,0:T(8,128)(2,1)S(1)}, u32[]{:S(2)}, u32[]{:S(2)}) collective-permute-start(bf16[2,128,512]{2,1,0:T(8,128)(2,1)S(1)} %get-tuple-element.34), channel_id=1, source_target_pairs={{0,12},{1,13},{36,32},{37,33},{72,68},{73,69},{108,104},{109,105},... | collective-permute-start | bytes 786440 | tf_op jit(solution)/shard_map/ppermute | solution.py:38
  22.5 1.5 collective-permute-start.17
  23.3 2.1 %collective-permute-start.5 = (bf16[2,128,512]{2,1,0:T(8,128)(2,1)S(1)}, bf16[2,128,512]{2,1,0:T(8,128)(2,1)S(1)}, u32[]{:S(2)}, u32[]{:S(2)}) collective-permute-start(bf16[2,128,512]{2,1,0:T(8,128)(2,1)S(1)} %fusion.3), channel_id=1, source_target_pairs={{0,14},{1,15},{12,10},{13,11},{32,46},{33,47},{36,34},{37,35},{68,... | collective-permute-start | bytes 786440 | tf_op jit(solution)/shard_map/ppermute | solution.py:38
  24.0 25.8 %collective-permute-start.20 = (bf16[2,128,512]{2,1,0:T(8,128)(2,1)S(1)}, bf16[2,128,512]{2,1,0:T(8,128)(2,1)S(1)}, u32[]{:S(2)}, u32[]{:S(2)}) collective-permute-start(bf16[2,128,512]{2,1,0:T(8,128)(2,1)S(1)} %fusion.4), channel_id=1, source_target_pairs={{0,192},{1,193},{2,194},{3,195},{4,196},{5,197},{6,198},{7,199},{3... | collective-permute-start | bytes 786440 | tf_op jit(solution)/shard_map/ppermute | solution.py:38
  25.4 27.7 %collective-permute-start.6 = (bf16[2,128,512]{2,1,0:T(8,128)(2,1)S(1)}, bf16[2,128,512]{2,1,0:T(8,128)(2,1)}, u32[]{:S(2)}, u32[]{:S(2)}) collective-permute-start(bf16[2,128,512]{2,1,0:T(8,128)(2,1)S(1)} %fusion.6), channel_id=1, source_target_pairs={{0,16},{1,17},{2,18},{3,19},{4,20},{5,21},{6,22},{7,23},{8,24},{9,... | collective-permute-start | bytes 786440 | tf_op jit(solution)/shard_map/ppermute | solution.py:38
  50.5 6.4 %collective-permute-start.18 = (bf16[2,128,512]{2,1,0:T(8,128)(2,1)S(1)}, bf16[2,128,512]{2,1,0:T(8,128)(2,1)S(1)}, u32[]{:S(2)}, u32[]{:S(2)}) collective-permute-start(bf16[2,128,512]{2,1,0:T(8,128)(2,1)S(1)} %get-tuple-element.50), channel_id=1, source_target_pairs={{0,64},{1,65},{2,66},{3,67},{4,68},{5,69},{6,70},{7,71},{32,96},{3... | collective-permute-start | bytes 786440 | tf_op jit(solution)/shard_map/ppermute | solution.py:38
  51.2 14.8 %collective-permute-start.21 = (bf16[2,128,512]{2,1,0:T(8,128)(2,1)}, bf16[2,128,512]{2,1,0:T(8,128)(2,1)}, u32[]{:S(2)}, u32[]{:S(2)}) collective-permute-start(bf16[2,128,512]{2,1,0:T(8,128)(2,1)} %get-tuple-element.49), channel_id=1, source_target_pairs={{0,192},{1,193},{2,194},{3,195},{4,196},{5,197},{6,198},{7,199},{8... | collective-permute-start | bytes 786440 | tf_op jit(solution)/shard_map/ppermute | solution.py:38
  54.9 9.1 %collective-permute-start.7 = (bf16[2,128,512]{2,1,0:T(8,128)(2,1)}, bf16[2,128,512]{2,1,0:T(8,128)(2,1)}, u32[]{:S(2)}, u32[]{:S(2)}) collective-permute-start(bf16[2,128,512]{2,1,0:T(8,128)(2,1)} %get-tuple-element.52), channel_id=1, source_target_pairs={{0,14},{1,15},{2,0},{3,1},{4,2},{5,3},{6,4},{7,5},{8,6},{9,7},{10,... | collective-permute-start | bytes 786440 | tf_op jit(solution)/shard_map/ppermute | solution.py:38
  56.1 9.9 %collective-permute-start.10 = (bf16[2,128,512]{2,1,0:T(8,128)(2,1)}, bf16[2,128,512]{2,1,0:T(8,128)(2,1)}, u32[]{:S(2)}, u32[]{:S(2)}) collective-permute-start(bf16[2,128,512]{2,1,0:T(8,128)(2,1)} %get-tuple-element.52), channel_id=1, source_target_pairs={{0,2},{1,3},{2,4},{3,5},{4,6},{5,7},{6,8},{7,9},{8,10},{9,11},{10,... | collective-permute-start | bytes 786440 | tf_op jit(solution)/shard_map/ppermute | solution.py:38
  57.7 8.4 %collective-permute-start.19 = (bf16[2,128,512]{2,1,0:T(8,128)(2,1)}, bf16[2,128,512]{2,1,0:T(8,128)(2,1)S(1)}, u32[]{:S(2)}, u32[]{:S(2)}) collective-permute-start(bf16[2,128,512]{2,1,0:T(8,128)(2,1)} %broadcast_select_fusion.3), channel_id=1, source_target_pairs={{0,64},{1,65},{2,66},{3,67},{4,68},{5,69},{6,70},{7,71},{24,88},{2... | collective-permute-start | bytes 786440 | tf_op jit(solution)/shard_map/ppermute | solution.py:38
  64.0 8.8 %collective-permute-start.8 = (bf16[2,128,512]{2,1,0:T(8,128)(2,1)}, bf16[2,128,512]{2,1,0:T(8,128)(2,1)S(1)}, u32[]{:S(2)}, u32[]{:S(2)}) collective-permute-start(bf16[2,128,512]{2,1,0:T(8,128)(2,1)} %collective-permute-done.7), channel_id=1, source_target_pairs={{0,14},{1,15},{2,0},{3,1},{4,2},{5,3},{6,4},{7,5},{8,6},{9,7},{10,... | collective-permute-start | bytes 786440 | tf_op jit(solution)/shard_map/ppermute | solution.py:38
  66.0 9.9 %collective-permute-start.11 = (bf16[2,128,512]{2,1,0:T(8,128)(2,1)}, bf16[2,128,512]{2,1,0:T(8,128)(2,1)S(1)}, u32[]{:S(2)}, u32[]{:S(2)}) collective-permute-start(bf16[2,128,512]{2,1,0:T(8,128)(2,1)} %collective-permute-done.10), channel_id=1, source_target_pairs={{0,2},{1,3},{2,4},{3,5},{4,6},{5,7},{6,8},{7,9},{8,10},{9,11},{10,... | collective-permute-start | bytes 786440 | tf_op jit(solution)/shard_map/ppermute | solution.py:38
  67.2 16.7 %collective-permute-start.22 = (bf16[2,2,128,512]{3,2,1,0:T(8,128)(2,1)S(1)}, bf16[2,2,128,512]{3,2,1,0:T(8,128)(2,1)S(1)}, u32[]{:S(2)}, u32[]{:S(2)}) collective-permute-start(bf16[2,2,128,512]{3,2,1,0:T(8,128)(2,1)S(1)} %pad_maximum_fusion.1), channel_id=1, source_target_pairs={{0,32},{1,33},{2,34},{3,35},{4,36},{5,37},{6,38},{7,39},{8,40},{9,... | collective-permute-start | bytes 1572872 | tf_op jit(solution)/shard_map/ppermute | solution.py:38
  72.8 7.8 %collective-permute-start.9 = (bf16[2,128,512]{2,1,0:T(8,128)(2,1)S(1)}, bf16[2,128,512]{2,1,0:T(8,128)(2,1)S(1)}, u32[]{:S(2)}, u32[]{:S(2)}) collective-permute-start(bf16[2,128,512]{2,1,0:T(8,128)(2,1)S(1)} %collective-permute-done.8), channel_id=1, source_target_pairs={{0,14},{1,15},{2,0},{3,1},{4,2},{5,3},{6,4},{7,5},{8,6},{9,7},{10,... | collective-permute-start | bytes 786440 | tf_op jit(solution)/shard_map/ppermute | solution.py:38
  75.9 7.9 %collective-permute-start.12 = (bf16[2,128,512]{2,1,0:T(8,128)(2,1)S(1)}, bf16[2,128,512]{2,1,0:T(8,128)(2,1)S(1)}, u32[]{:S(2)}, u32[]{:S(2)}) collective-permute-start(bf16[2,128,512]{2,1,0:T(8,128)(2,1)S(1)} %collective-permute-done.11), channel_id=1, source_target_pairs={{0,2},{1,3},{2,4},{3,5},{4,6},{5,7},{6,8},{7,9},{8,10},{9,11},{10,... | collective-permute-start | bytes 786440 | tf_op jit(solution)/shard_map/ppermute | solution.py:38
  80.6 17.0 %collective-permute-start.14 = (bf16[128,512]{1,0:T(8,128)(2,1)S(1)}, bf16[128,512]{1,0:T(8,128)(2,1)S(1)}, u32[]{:S(2)}, u32[]{:S(2)}) collective-permute-start(bf16[128,512]{1,0:T(8,128)(2,1)S(1)} %slice_bitcast_fusion), channel_id=1, source_target_pairs={{0,14},{1,15},{2,0},{3,1},{4,2},{5,3},{6,4},{7,5},{8,6},{9,7},{10,... | collective-permute-start | bytes 393224 | tf_op jit(solution)/shard_map/ppermute | solution.py:38
  83.8 2.2 %copy-start.1 = (f32[2048,512]{1,0:T(8,128)S(1)}, f32[2048,512]{1,0:T(8,128)}, u32[]{:S(2)}) copy-start(f32[2048,512]{1,0:T(8,128)} %block_ref.1) | copy-start | bytes 12582916
  83.8 13.8 %collective-permute-start.13 = (bf16[128,512]{1,0:T(8,128)(2,1)S(1)}, bf16[128,512]{1,0:T(8,128)(2,1)S(1)}, u32[]{:S(2)}, u32[]{:S(2)}) collective-permute-start(bf16[128,512]{1,0:T(8,128)(2,1)S(1)} %slice_bitcast_fusion.1), channel_id=1, source_target_pairs={{0,2},{1,3},{2,4},{3,5},{4,6},{5,7},{6,8},{7,9},{8,10},{9,11},{10,... | collective-permute-start | bytes 393224 | tf_op jit(solution)/shard_map/ppermute | solution.py:38
  88.4 19.7 %collective-permute-start.23 = (bf16[2048,256]{1,0:T(8,128)(2,1)S(1)}, bf16[2048,256]{1,0:T(8,128)(2,1)S(1)}, u32[]{:S(2)}, u32[]{:S(2)}) collective-permute-start(bf16[2048,256]{1,0:T(8,128)(2,1)S(1)} %get-tuple-element.39.refs_0_), channel_id=1, source_target_pairs={{0,1},{1,2},{2,3},{3,4},{4,5},{5,6},{6,7},{7,8},{8,9},{9,10},{10,1... | collective-permute-start | bytes 3145736 | tf_op jit(solution)/shard_map/ppermute | solution.py:38
  90.3 19.6 %collective-permute-start.24 = (bf16[2048,256]{1,0:T(8,128)(2,1)S(1)}, bf16[2048,256]{1,0:T(8,128)(2,1)S(1)}, u32[]{:S(2)}, u32[]{:S(2)}) collective-permute-start(bf16[2048,256]{1,0:T(8,128)(2,1)S(1)} %get-tuple-element.40.refs_1_), channel_id=1, source_target_pairs={{1,0},{2,1},{3,2},{4,3},{5,4},{6,5},{7,6},{8,7},{9,8},{10,9},{11,1... | collective-permute-start | bytes 3145736 | tf_op jit(solution)/shard_map/ppermute | solution.py:38
  98.7 36.7 %collective-permute-start.15 = (bf16[8,2,128,512]{3,2,1,0:T(8,128)(2,1)S(1)}, bf16[8,2,128,512]{3,2,1,0:T(8,128)(2,1)S(1)}, u32[]{:S(2)}, u32[]{:S(2)}) collective-permute-start(bf16[8,2,128,512]{3,2,1,0:T(8,128)(2,1)S(1)} %bitcast_dynamic-update-slice_fusion.refs_1_), channel_id=1, source_target_pairs={{0,1},{1,0},{2,3},{3,2},{4,5},{5,4},{6,7},{7,6},{8,9},{9,8},{10,11... | collective-permute-start | bytes 6291464 | tf_op jit(solution)/shard_map/ppermute | solution.py:38
  112.3 22.8 %collective-permute-start.25 = (bf16[2048,256]{1,0:T(8,128)(2,1)S(1)}, bf16[2048,256]{1,0:T(8,128)(2,1)S(1)}, u32[]{:S(2)}, u32[]{:S(2)}) collective-permute-start(bf16[2048,256]{1,0:T(8,128)(2,1)S(1)} %get-tuple-element.41.refs_3_), channel_id=1, source_target_pairs={{0,1},{1,2},{2,3},{3,4},{4,5},{5,6},{6,7},{7,8},{8,9},{9,10},{10,1... | collective-permute-start | bytes 3145736 | tf_op jit(solution)/shard_map/ppermute | solution.py:38
  114.2 21.1 %collective-permute-start.26 = (bf16[2048,256]{1,0:T(8,128)(2,1)S(1)}, bf16[2048,256]{1,0:T(8,128)(2,1)S(1)}, u32[]{:S(2)}, u32[]{:S(2)}) collective-permute-start(bf16[2048,256]{1,0:T(8,128)(2,1)S(1)} %get-tuple-element.42.refs_4_), channel_id=1, source_target_pairs={{1,0},{2,1},{3,2},{4,3},{5,4},{6,5},{7,6},{8,7},{9,8},{10,9},{11,1... | collective-permute-start | bytes 3145736 | tf_op jit(solution)/shard_map/ppermute | solution.py:38
  137.1 11.8 %collective-permute-start.27 = (bf16[256,512]{1,0:T(8,128)(2,1)S(1)}, bf16[256,512]{1,0:T(8,128)(2,1)S(1)}, u32[]{:S(2)}, u32[]{:S(2)}) collective-permute-start(bf16[256,512]{1,0:T(8,128)(2,1)S(1)} %get-tuple-element.44), channel_id=1, source_target_pairs={{0,32},{1,33},{2,34},{3,35},{4,36},{5,37},{6,38},{7,39},{8,40},{9,... | collective-permute-start | bytes 786440 | tf_op jit(solution)/shard_map/ppermute | solution.py:38
  144.6 11.6 %collective-permute-start.28 = (bf16[256,512]{1,0:T(8,128)(2,1)S(1)}, bf16[256,512]{1,0:T(8,128)(2,1)S(1)}, u32[]{:S(2)}, u32[]{:S(2)}) collective-permute-start(bf16[256,512]{1,0:T(8,128)(2,1)S(1)} %get-tuple-element.45), channel_id=1, source_target_pairs={{32,0},{33,1},{34,2},{35,3},{36,4},{37,5},{38,6},{39,7},{40,8},{41... | collective-permute-start | bytes 786440 | tf_op jit(solution)/shard_map/ppermute | solution.py:38
  158.9 10.4 %collective-permute-start.29 = (bf16[256,512]{1,0:T(8,128)(2,1)S(1)}, bf16[256,512]{1,0:T(8,128)(2,1)S(1)}, u32[]{:S(2)}, u32[]{:S(2)}) collective-permute-start(bf16[256,512]{1,0:T(8,128)(2,1)S(1)} %get-tuple-element.46), channel_id=1, source_target_pairs={{0,32},{1,33},{2,34},{3,35},{4,36},{5,37},{6,38},{7,39},{8,40},{9,... | collective-permute-start | bytes 786440 | tf_op jit(solution)/shard_map/ppermute | solution.py:38
  164.8 9.2 %collective-permute-start.30 = (bf16[256,512]{1,0:T(8,128)(2,1)S(1)}, bf16[256,512]{1,0:T(8,128)(2,1)S(1)}, u32[]{:S(2)}, u32[]{:S(2)}) collective-permute-start(bf16[256,512]{1,0:T(8,128)(2,1)S(1)} %get-tuple-element.47), channel_id=1, source_target_pairs={{32,0},{33,1},{34,2},{35,3},{36,4},{37,5},{38,6},{39,7},{40,8},{41... | collective-permute-start | bytes 786440 | tf_op jit(solution)/shard_map/ppermute | solution.py:38
where the time goes:
time: 176 us
  waiting for transfers between devices  77.2 us (44%)
  starting transfers between devices  65.9 us (37%)
  Pallas kernels  18.4 us (10%)
  local copies, waits for them, and re-layouts  6.81 us (4%)
  other arithmetic  6.66 us (4%)
    ppermute x31, waiting for transfers between devices, move(): return lax.ppermute(value, ALL, pairs)  77.2 us
    ppermute x31, starting transfers between devices, move(): return lax.ppermute(value, ALL, pairs)  65.9 us
    pallas_call x10, Pallas kernels, call(): pl.pallas_call(body, grid_spec=pltpu.PrefetchScalarGridSpec(num_scalar_pr...  18.4 us
    unnamed x9, local copies, waits for them, and re-layouts  5.13 us
  transfers between devices with their start and end apart: 31, of which 13 were waited for; matrix products, arithmetic and copies ran while one was open for 5% of the time, Pallas kernels for 6%

commit v1 on v0

--- a/solution.py
+++ b/solution.py
@@ -312,18 +312,23 @@
     store_halves(flags, product, right_ref, left_ref)
 
 
-def right(flags, sources, rot, slot):
+def right(flags, sources, rot, slot, pairs):
+    base, stride = pairs
     out = pl.BlockSpec((N, H), lambda i, f: (i, 0))
     first = slot == 0
     return call(
         right_one_body if first else right_two_body,
         flags,
         (*sources, rot),
-        ([pl.BlockSpec((N, N), lambda i, f: (i, 0))] if first else half_specs(0, 1))
+        (
+            [pl.BlockSpec((N, N), lambda i, f: (base + stride * i, 0))]
+            if first
+            else half_specs(0, 1)
+        )
         + [pl.BlockSpec((4, 1, Q, N), lambda i, f: (0, slot, 0, 0))],
         [out, out],
-        [shape(GROUP * N, H)] * 2,
-        (GROUP,),
+        [shape(2 * N, H)] * 2,
+        (2,),
         name="right",
     )
 
@@ -413,7 +418,7 @@
     edge = pairs == EDGE
     pieces = pl.BlockSpec((8, 1, Q, N), lambda i, f: (0, slot, 0, 0))
     if slot == 0:
-        specs = half_specs(base, stride)
+        specs = half_specs(0, 1)
     else:
         specs = [pl.BlockSpec((N, N), lambda i, f: (base + stride * i, 0))]
     specs = specs + [whole((H, N))] * len(ends)
@@ -544,21 +549,25 @@
     cols = jnp.concatenate(
         [jnp.where(dy == 0, mine, other), jnp.where(dy == 0, other, mine)], 0
     )
-    halves = right(flags, (factor,), cols, 0)
+    edge = right(flags, (factor,), cols, 0, EDGE)
+    edge = exchange_columns(edge)
     ring()
-    halves = exchange_columns(halves)
+    inner = right(flags, (factor,), cols, 0, INNER)
+    inner = exchange_columns(inner)
     last = (move(ahead[3][0], z_pairs(1)), move(behind[3][1], z_pairs(-1)))
-    halves = right(flags, halves, cols, 1)
-    halves = exchange_columns(halves)
+    edge = right(flags, edge, cols, 1, EDGE)
+    edge = exchange_columns(edge)
+    inner = right(flags, inner, cols, 1, INNER)
+    inner = exchange_columns(inner)
     line = jnp.stack(
         [piece, *behind[1:], jnp.stack(last), ahead[3], ahead[2], ahead[1]]
     )
     rows = line, move(line, CORE_SWAP)
 
-    main, down, up = left(flags, rows, 0, EDGE, halves)
+    main, down, up = left(flags, rows, 0, EDGE, edge)
     above = move(down, ROW_DOWN)
     below = move(up, ROW_UP)
-    (main,) = left(flags, rows, 0, INNER, halves, target=main)
+    (main,) = left(flags, rows, 0, INNER, inner, target=main)
     out, down, up = left(flags, rows, 1, EDGE, (main,), (above, below))
     last_above = move(down, ROW_DOWN)
     last_below = move(up, ROW_UP)

time: 176 us -> 184 us (1.045)
  the two profiles are of different devices: /device:TPU:26 before, /device:TPU:7 now
where the time goes in v1:
time: 184 us; the launch traced here: 183 us
  waiting for transfers between devices  97.3 us (53%)
  starting transfers between devices  55.1 us (30%)
  Pallas kernels  19.7 us (11%)
  other arithmetic  5.71 us (3%)
  local copies, waits for them, and re-layouts  4.92 us (3%)
    ppermute x35, waiting for transfers between devices, move(): return lax.ppermute(value, ALL, pairs)  97.3 us
    ppermute x35, starting transfers between devices, move(): return lax.ppermute(value, ALL, pairs)  55.1 us
    pallas_call x12, Pallas kernels, call(): pl.pallas_call(body, grid_spec=pltpu.PrefetchScalarGridSpec(num_scalar_pr...  19.7 us
  transfers between devices with their start and end apart: 35, of which 16 were waited for; matrix products, arithmetic and copies ran while one was open for 4% of the time, Pallas kernels for 8%

profile of v1, /device:TPU:7, one launch (start us, length us, event | category | flops | bytes accessed | tf_op | source)
XLA Modules:
  0.0 183.5 jit_solution(9493165416099720496)
XLA Ops:
  0.7 2.2 %copy-done = f32[2048,512]{1,0:T(8,128)S(1)} copy-done((f32[2048,512]{1,0:T(8,128)S(1)}, f32[2048,512]{1,0:T(8,128)}, u32[]{:S(2)}) %copy-start) | copy-done | bytes 4194328
  2.9 1.5 cross_block.1
  5.1 1.3 solve_one.1
  7.7 1.4 collective-permute-start
  9.1 1.4 collective-permute-start.16
  14.3 1.3 collective-permute-start.20
  15.7 1.3 collective-permute-start.6
  17.0 25.0 %collective-permute-done.20 = bf16[2,128,512]{2,1,0:T(8,128)(2,1)S(1)} collective-permute-done((bf16[2,128,512]{2,1,0:T(8,128)(2,1)S(1)}, bf16[2,128,512]{2,1,0:T(8,128)(2,1)S(1)}, u32[]{:S(2)}, u32[]{:S(2)}) %collective-permute-start.20) | collective-permute-done | bytes 262176 | tf_op jit(solution)/shard_map/ppermute | solution.py:38
  43.5 1.9 %collective-permute-start.21 = (bf16[2,128,512]{2,1,0:T(8,128)(2,1)}, bf16[2,128,512]{2,1,0:T(8,128)(2,1)}, u32[]{:S(2)}, u32[]{:S(2)}) collective-permute-start(bf16[2,128,512]{2,1,0:T(8,128)(2,1)} %get-tuple-element.57), channel_id=1, source_target_pairs={{0,192},{1,193},{2,194},{3,195},{4,196},{5,197},{6,198},{7,199},{8... | collective-permute-start | bytes 786440 | tf_op jit(solution)/shard_map/ppermute | solution.py:38
  45.4 11.6 %collective-permute-done.6 = bf16[2,128,512]{2,1,0:T(8,128)(2,1)} collective-permute-done((bf16[2,128,512]{2,1,0:T(8,128)(2,1)S(1)}, bf16[2,128,512]{2,1,0:T(8,128)(2,1)}, u32[]{:S(2)}, u32[]{:S(2)}) %collective-permute-start.6) | collective-permute-done | bytes 262176 | tf_op jit(solution)/shard_map/ppermute | solution.py:38
  57.1 1.8 bitcast_dynamic-update-slice_fusion.6
  58.8 1.5 collective-permute-start.10
  61.7 5.1 %collective-permute-done.7 = bf16[2,128,512]{2,1,0:T(8,128)(2,1)} collective-permute-done((bf16[2,128,512]{2,1,0:T(8,128)(2,1)}, bf16[2,128,512]{2,1,0:T(8,128)(2,1)}, u32[]{:S(2)}, u32[]{:S(2)}) %collective-permute-start.7) | collective-permute-done | bytes 262176 | tf_op jit(solution)/shard_map/ppermute | solution.py:38
  66.8 1.5 collective-permute-start.11
  69.3 4.5 %collective-permute-done.8 = bf16[2,128,512]{2,1,0:T(8,128)(2,1)S(1)} collective-permute-done((bf16[2,128,512]{2,1,0:T(8,128)(2,1)}, bf16[2,128,512]{2,1,0:T(8,128)(2,1)S(1)}, u32[]{:S(2)}, u32[]{:S(2)}) %collective-permute-start.8) | collective-permute-done | bytes 262176 | tf_op jit(solution)/shard_map/ppermute | solution.py:38
  73.8 1.5 collective-permute-start.9
  76.5 3.2 %collective-permute-done.9 = bf16[2,128,512]{2,1,0:T(8,128)(2,1)S(1)} collective-permute-done((bf16[2,128,512]{2,1,0:T(8,128)(2,1)S(1)}, bf16[2,128,512]{2,1,0:T(8,128)(2,1)S(1)}, u32[]{:S(2)}, u32[]{:S(2)}) %collective-permute-start.9) | collective-permute-done | bytes 262176 | tf_op jit(solution)/shard_map/ppermute | solution.py:38
  79.7 3.1 %collective-permute-start.14 = (bf16[128,512]{1,0:T(8,128)(2,1)S(1)}, bf16[128,512]{1,0:T(8,128)(2,1)S(1)}, u32[]{:S(2)}, u32[]{:S(2)}) collective-permute-start(bf16[128,512]{1,0:T(8,128)(2,1)S(1)} %slice_bitcast_fusion), channel_id=1, source_target_pairs={{0,14},{1,15},{2,0},{3,1},{4,2},{5,3},{6,4},{7,5},{8,6},{9,7},{10,... | collective-permute-start | bytes 393224 | tf_op jit(solution)/shard_map/ppermute | solution.py:38
  84.7 4.0 %collective-permute-done.13 = bf16[128,512]{1,0:T(8,128)(2,1)S(1)} collective-permute-done((bf16[128,512]{1,0:T(8,128)(2,1)S(1)}, bf16[128,512]{1,0:T(8,128)(2,1)S(1)}, u32[]{:S(2)}, u32[]{:S(2)}) %collective-permute-start.13) | collective-permute-done | bytes 131104 | tf_op jit(solution)/shard_map/ppermute | solution.py:38
  89.8 4.0 %collective-permute-start.15 = (bf16[8,2,128,512]{3,2,1,0:T(8,128)(2,1)S(1)}, bf16[8,2,128,512]{3,2,1,0:T(8,128)(2,1)S(1)}, u32[]{:S(2)}, u32[]{:S(2)}) collective-permute-start(bf16[8,2,128,512]{3,2,1,0:T(8,128)(2,1)S(1)} %bitcast_dynamic-update-slice_fusion.refs_1_), channel_id=1, source_target_pairs={{0,1},{1,0},{2,3},{3,2},{4,5},{5,4},{6,7},{7,6},{8,9},{9,8},{10,11... | collective-permute-start | bytes 6291464 | tf_op jit(solution)/shard_map/ppermute | solution.py:38
  94.0 13.4 %collective-permute-done.22 = bf16[2,2,128,512]{3,2,1,0:T(8,128)(2,1)S(1)} collective-permute-done((bf16[2,2,128,512]{3,2,1,0:T(8,128)(2,1)S(1)}, bf16[2,2,128,512]{3,2,1,0:T(8,128)(2,1)S(1)}, u32[]{:S(2)}, u32[]{:S(2)}) %collective-permute-start.22) | collective-permute-done | bytes 524320 | tf_op jit(solution)/shard_map/ppermute | solution.py:38
  107.6 1.5 right.6
  109.1 1.9 %collective-permute-start.27 = (bf16[1024,256]{1,0:T(8,128)(2,1)S(1)}, bf16[1024,256]{1,0:T(8,128)(2,1)S(1)}, u32[]{:S(2)}, u32[]{:S(2)}) collective-permute-start(bf16[1024,256]{1,0:T(8,128)(2,1)S(1)} %get-tuple-element.47.refs_0_), channel_id=1, source_target_pairs={{0,1},{1,2},{2,3},{3,4},{4,5},{5,6},{6,7},{7,8},{8,9},{9,10},{10,1... | collective-permute-start | bytes 1572872 | tf_op jit(solution)/shard_map/ppermute | solution.py:38
  111.1 2.4 %collective-permute-start.28 = (bf16[1024,256]{1,0:T(8,128)(2,1)S(1)}, bf16[1024,256]{1,0:T(8,128)(2,1)S(1)}, u32[]{:S(2)}, u32[]{:S(2)}) collective-permute-start(bf16[1024,256]{1,0:T(8,128)(2,1)S(1)} %get-tuple-element.48.refs_1_), channel_id=1, source_target_pairs={{1,0},{2,1},{3,2},{4,3},{5,4},{6,5},{7,6},{8,7},{9,8},{10,9},{11,1... | collective-permute-start | bytes 1572872 | tf_op jit(solution)/shard_map/ppermute | solution.py:38
  113.5 1.5 right.4
  115.0 3.1 %collective-permute-start.23 = (bf16[1024,256]{1,0:T(8,128)(2,1)S(1)}, bf16[1024,256]{1,0:T(8,128)(2,1)S(1)}, u32[]{:S(2)}, u32[]{:S(2)}) collective-permute-start(bf16[1024,256]{1,0:T(8,128)(2,1)S(1)} %get-tuple-element.43.refs_0_), channel_id=1, source_target_pairs={{0,1},{1,2},{2,3},{3,4},{4,5},{5,6},{6,7},{7,8},{8,9},{9,10},{10,1... | collective-permute-start | bytes 1572872 | tf_op jit(solution)/shard_map/ppermute | solution.py:38
  118.2 1.9 %collective-permute-start.24 = (bf16[1024,256]{1,0:T(8,128)(2,1)S(1)}, bf16[1024,256]{1,0:T(8,128)(2,1)S(1)}, u32[]{:S(2)}, u32[]{:S(2)}) collective-permute-start(bf16[1024,256]{1,0:T(8,128)(2,1)S(1)} %get-tuple-element.44.refs_1_), channel_id=1, source_target_pairs={{1,0},{2,1},{3,2},{4,3},{5,4},{6,5},{7,6},{8,7},{9,8},{10,9},{11,1... | collective-permute-start | bytes 1572872 | tf_op jit(solution)/shard_map/ppermute | solution.py:38
  120.1 1.5 collective-permute-done.28.refs_3_
  121.6 1.5 right.7
  123.1 2.2 %collective-permute-start.29 = (bf16[1024,256]{1,0:T(8,128)(2,1)S(1)}, bf16[1024,256]{1,0:T(8,128)(2,1)S(1)}, u32[]{:S(2)}, u32[]{:S(2)}) collective-permute-start(bf16[1024,256]{1,0:T(8,128)(2,1)S(1)} %get-tuple-element.49.refs_3_), channel_id=1, source_target_pairs={{0,1},{1,2},{2,3},{3,4},{4,5},{5,6},{6,7},{7,8},{8,9},{9,10},{10,1... | collective-permute-start | bytes 1572872 | tf_op jit(solution)/shard_map/ppermute | solution.py:38
  125.3 2.2 %collective-permute-start.30 = (bf16[1024,256]{1,0:T(8,128)(2,1)S(1)}, bf16[1024,256]{1,0:T(8,128)(2,1)S(1)}, u32[]{:S(2)}, u32[]{:S(2)}) collective-permute-start(bf16[1024,256]{1,0:T(8,128)(2,1)S(1)} %get-tuple-element.50.refs_4_), channel_id=1, source_target_pairs={{1,0},{2,1},{3,2},{4,3},{5,4},{6,5},{7,6},{8,7},{9,8},{10,9},{11,1... | collective-permute-start | bytes 1572872 | tf_op jit(solution)/shard_map/ppermute | solution.py:38
  128.7 1.5 right.5
  130.2 2.2 %collective-permute-start.25 = (bf16[1024,256]{1,0:T(8,128)(2,1)S(1)}, bf16[1024,256]{1,0:T(8,128)(2,1)S(1)}, u32[]{:S(2)}, u32[]{:S(2)}) collective-permute-start(bf16[1024,256]{1,0:T(8,128)(2,1)S(1)} %get-tuple-element.45.refs_3_), channel_id=1, source_target_pairs={{0,1},{1,2},{2,3},{3,4},{4,5},{5,6},{6,7},{7,8},{8,9},{9,10},{10,1... | collective-permute-start | bytes 1572872 | tf_op jit(solution)/shard_map/ppermute | solution.py:38
  132.4 2.1 %collective-permute-start.26 = (bf16[1024,256]{1,0:T(8,128)(2,1)S(1)}, bf16[1024,256]{1,0:T(8,128)(2,1)S(1)}, u32[]{:S(2)}, u32[]{:S(2)}) collective-permute-start(bf16[1024,256]{1,0:T(8,128)(2,1)S(1)} %get-tuple-element.46.refs_4_), channel_id=1, source_target_pairs={{1,0},{2,1},{3,2},{4,3},{5,4},{6,5},{7,6},{8,7},{9,8},{10,9},{11,1... | collective-permute-start | bytes 1572872 | tf_op jit(solution)/shard_map/ppermute | solution.py:38
  134.5 1.2 collective-permute-done.30.refs_6_
  135.8 1.8 left_edge.2
  137.6 2.2 %collective-permute-start.31 = (bf16[256,512]{1,0:T(8,128)(2,1)S(1)}, bf16[256,512]{1,0:T(8,128)(2,1)S(1)}, u32[]{:S(2)}, u32[]{:S(2)}) collective-permute-start(bf16[256,512]{1,0:T(8,128)(2,1)S(1)} %get-tuple-element.52), channel_id=1, source_target_pairs={{0,32},{1,33},{2,34},{3,35},{4,36},{5,37},{6,38},{7,39},{8,40},{9,... | collective-permute-start | bytes 786440 | tf_op jit(solution)/shard_map/ppermute | solution.py:38
  139.7 4.0 %collective-permute-start.32 = (bf16[256,512]{1,0:T(8,128)(2,1)S(1)}, bf16[256,512]{1,0:T(8,128)(2,1)S(1)}, u32[]{:S(2)}, u32[]{:S(2)}) collective-permute-start(bf16[256,512]{1,0:T(8,128)(2,1)S(1)} %get-tuple-element.53), channel_id=1, source_target_pairs={{32,0},{33,1},{34,2},{35,3},{36,4},{37,5},{38,6},{39,7},{40,8},{41... | collective-permute-start | bytes 786440 | tf_op jit(solution)/shard_map/ppermute | solution.py:38
  143.8 1.8 left_inner.2.refs_3_
  145.5 6.1 %collective-permute-done.31.refs_4_ = bf16[256,512]{1,0:T(8,128)(2,1)S(1)} collective-permute-done((bf16[256,512]{1,0:T(8,128)(2,1)S(1)}, bf16[256,512]{1,0:T(8,128)(2,1)S(1)}, u32[]{:S(2)}, u32[]{:S(2)}) %collective-permute-start.31) | collective-permute-done | bytes 262176 | tf_op jit(solution)/shard_map/ppermute | solution.py:38
  151.6 10.8 %collective-permute-done.32.refs_5_ = bf16[256,512]{1,0:T(8,128)(2,1)S(1)} collective-permute-done((bf16[256,512]{1,0:T(8,128)(2,1)S(1)}, bf16[256,512]{1,0:T(8,128)(2,1)S(1)}, u32[]{:S(2)}, u32[]{:S(2)}) %collective-permute-start.32) | collective-permute-done | bytes 262176 | tf_op jit(solution)/shard_map/ppermute | solution.py:38
  162.4 2.7 %left_edge.3 = (f32[2048,512]{1,0:T(8,128)}, bf16[256,512]{1,0:T(8,128)(2,1)S(1)}, bf16[256,512]{1,0:T(8,128)(2,1)S(1)}) custom-call(s32[16]{0:T(128)S(1)} %dynamic-slice_bitcast_fusion.flags.refs_0_, bf16[8,2,128,512]{3,2,1,0:T(8,128)(2,1)S(1)} %bitcast_dynamic-update-slice_fusion.refs_1_, bf16[8,2,128,512]{3,2,1,0:T(8,128)(2,1)S(1)} %collective-permute-done.15.refs_2_, ...), custom_call_target="tpu_custom_call" | custom-call | tf_op jit(solution)/shard_map/left_edge/pallas_call | solution.py:199
  165.1 1.9 %collective-permute-start.33 = (bf16[256,512]{1,0:T(8,128)(2,1)S(1)}, bf16[256,512]{1,0:T(8,128)(2,1)S(1)}, u32[]{:S(2)}, u32[]{:S(2)}) collective-permute-start(bf16[256,512]{1,0:T(8,128)(2,1)S(1)} %get-tuple-element.54), channel_id=1, source_target_pairs={{0,32},{1,33},{2,34},{3,35},{4,36},{5,37},{6,38},{7,39},{8,40},{9,... | collective-permute-start | bytes 786440 | tf_op jit(solution)/shard_map/ppermute | solution.py:38
  167.0 4.3 %collective-permute-start.34 = (bf16[256,512]{1,0:T(8,128)(2,1)S(1)}, bf16[256,512]{1,0:T(8,128)(2,1)S(1)}, u32[]{:S(2)}, u32[]{:S(2)}) collective-permute-start(bf16[256,512]{1,0:T(8,128)(2,1)S(1)} %get-tuple-element.55), channel_id=1, source_target_pairs={{32,0},{33,1},{34,2},{35,3},{36,4},{37,5},{38,6},{39,7},{40,8},{41... | collective-permute-start | bytes 786440 | tf_op jit(solution)/shard_map/ppermute | solution.py:38
  171.3 2.6 %left_inner.3.main_ref = f32[2048,512]{1,0:T(8,128)} custom-call(s32[16]{0:T(128)S(1)} %dynamic-slice_bitcast_fusion.flags.refs_0_, bf16[8,2,128,512]{3,2,1,0:T(8,128)(2,1)S(1)} %bitcast_dynamic-update-slice_fusion.refs_1_, bf16[8,2,128,512]{3,2,1,0:T(8,128)(2,1)S(1)} %collective-permute-done.15.refs_2_, ...), custom_call_target="tpu_custom_call", output_to_operand_aliasing={{}: (4, {})} | custom-call | tf_op jit(solution)/shard_map/left_inner/pallas_call | solution.py:199
  173.9 1.5 collective-permute-done.33.above_ref
  175.4 6.3 %collective-permute-done.34.below_ref = bf16[256,512]{1,0:T(8,128)(2,1)S(1)} collective-permute-done((bf16[256,512]{1,0:T(8,128)(2,1)S(1)}, bf16[256,512]{1,0:T(8,128)(2,1)S(1)}, u32[]{:S(2)}, u32[]{:S(2)}) %collective-permute-start.34) | collective-permute-done | bytes 262176 | tf_op jit(solution)/shard_map/ppermute | solution.py:38
  181.8 1.6 settle.1
  (62 shorter events, 16.2 us)
Async XLA Ops:
  0.7 2.2 %copy-start = (f32[2048,512]{1,0:T(8,128)S(1)}, f32[2048,512]{1,0:T(8,128)}, u32[]{:S(2)}) copy-start(f32[2048,512]{1,0:T(8,128)} %block_ref.3) | copy-start | bytes 12582916
  4.4 6.1 %collective-permute-start.3 = (bf16[512,512]{1,0:T(8,128)(2,1)}, bf16[512,512]{1,0:T(8,128)(2,1)S(1)}, u32[]{:S(2)}, u32[]{:S(2)}) collective-permute-start(bf16[512,512]{1,0:T(8,128)(2,1)} %get-tuple-element.35), channel_id=1, source_target_pairs={{1,0},{2,1},{3,2},{4,3},{5,36},{38,37},{39,38},{40,39},{41,72},{74... | collective-permute-start | bytes 1572872 | tf_op jit(solution)/shard_map/ppermute | solution.py:38
  6.3 4.2 %collective-permute-start.1 = (bf16[768,256]{1,0:T(8,128)(2,1)S(1)}, bf16[768,256]{1,0:T(8,128)(2,1)S(1)}, u32[]{:S(2)}, u32[]{:S(2)}) collective-permute-start(bf16[768,256]{1,0:T(8,128)(2,1)S(1)} %get-tuple-element.33.own_right), channel_id=1, source_target_pairs={{0,1},{1,2},{2,3},{3,36},{36,37},{37,38},{38,39},{39,72},{72,73},{... | collective-permute-start | bytes 1179656 | tf_op jit(solution)/shard_map/ppermute | solution.py:38
  7.0 3.5 %collective-permute-start.2 = (bf16[768,256]{1,0:T(8,128)(2,1)S(1)}, bf16[768,256]{1,0:T(8,128)(2,1)S(1)}, u32[]{:S(2)}, u32[]{:S(2)}) collective-permute-start(bf16[768,256]{1,0:T(8,128)(2,1)S(1)} %get-tuple-element.34.own_left), channel_id=1, source_target_pairs={{1,0},{2,1},{3,2},{36,3},{37,36},{38,37},{39,38},{72,39},{73,72},{... | collective-permute-start | bytes 1179656 | tf_op jit(solution)/shard_map/ppermute | solution.py:38
  7.7 4.0 %collective-permute-start = (bf16[2,128,512]{2,1,0:T(8,128)(2,1)}, bf16[2,128,512]{2,1,0:T(8,128)(2,1)}, u32[]{:S(2)}, u32[]{:S(2)}) collective-permute-start(bf16[2,128,512]{2,1,0:T(8,128)(2,1)} %get-tuple-element.32), channel_id=1, source_target_pairs={{0,12},{1,13},{36,32},{37,33},{72,68},{73,69},{108,104},{109,105},... | collective-permute-start | bytes 786440 | tf_op jit(solution)/shard_map/ppermute | solution.py:38
  9.1 3.6 %collective-permute-start.16 = (bf16[2,128,512]{2,1,0:T(8,128)(2,1)S(1)}, bf16[2,128,512]{2,1,0:T(8,128)(2,1)}, u32[]{:S(2)}, u32[]{:S(2)}) collective-permute-start(bf16[2,128,512]{2,1,0:T(8,128)(2,1)S(1)} %get-tuple-element.40), channel_id=1, source_target_pairs={{0,32},{1,33},{2,34},{3,35},{36,4},{37,5},{38,6},{39,7},{72,104},{... | collective-permute-start | bytes 786440 | tf_op jit(solution)/shard_map/ppermute | solution.py:38
  11.1 2.4 %collective-permute-start.4 = (bf16[2,128,512]{2,1,0:T(8,128)(2,1)S(1)}, bf16[2,128,512]{2,1,0:T(8,128)(2,1)S(1)}, u32[]{:S(2)}, u32[]{:S(2)}) collective-permute-start(bf16[2,128,512]{2,1,0:T(8,128)(2,1)S(1)} %get-tuple-element.38), channel_id=1, source_target_pairs={{0,12},{1,13},{36,32},{37,33},{72,68},{73,69},{108,104},{109,105},... | collective-permute-start | bytes 786440 | tf_op jit(solution)/shard_map/ppermute | solution.py:38
  12.8 1.5 collective-permute-start.17
  13.6 2.1 %collective-permute-start.5 = (bf16[2,128,512]{2,1,0:T(8,128)(2,1)S(1)}, bf16[2,128,512]{2,1,0:T(8,128)(2,1)S(1)}, u32[]{:S(2)}, u32[]{:S(2)}) collective-permute-start(bf16[2,128,512]{2,1,0:T(8,128)(2,1)S(1)} %fusion.3), channel_id=1, source_target_pairs={{0,14},{1,15},{12,10},{13,11},{32,46},{33,47},{36,34},{37,35},{68,... | collective-permute-start | bytes 786440 | tf_op jit(solution)/shard_map/ppermute | solution.py:38
  14.3 27.7 %collective-permute-start.20 = (bf16[2,128,512]{2,1,0:T(8,128)(2,1)S(1)}, bf16[2,128,512]{2,1,0:T(8,128)(2,1)S(1)}, u32[]{:S(2)}, u32[]{:S(2)}) collective-permute-start(bf16[2,128,512]{2,1,0:T(8,128)(2,1)S(1)} %fusion.4), channel_id=1, source_target_pairs={{0,192},{1,193},{2,194},{3,195},{4,196},{5,197},{6,198},{7,199},{3... | collective-permute-start | bytes 786440 | tf_op jit(solution)/shard_map/ppermute | solution.py:38
  15.7 41.3 %collective-permute-start.6 = (bf16[2,128,512]{2,1,0:T(8,128)(2,1)S(1)}, bf16[2,128,512]{2,1,0:T(8,128)(2,1)}, u32[]{:S(2)}, u32[]{:S(2)}) collective-permute-start(bf16[2,128,512]{2,1,0:T(8,128)(2,1)S(1)} %fusion.6), channel_id=1, source_target_pairs={{0,16},{1,17},{2,18},{3,19},{4,20},{5,21},{6,22},{7,23},{8,24},{9,... | collective-permute-start | bytes 786440 | tf_op jit(solution)/shard_map/ppermute | solution.py:38
  42.8 17.5 %collective-permute-start.18 = (bf16[2,128,512]{2,1,0:T(8,128)(2,1)S(1)}, bf16[2,128,512]{2,1,0:T(8,128)(2,1)S(1)}, u32[]{:S(2)}, u32[]{:S(2)}) collective-permute-start(bf16[2,128,512]{2,1,0:T(8,128)(2,1)S(1)} %get-tuple-element.58), channel_id=1, source_target_pairs={{0,64},{1,65},{2,66},{3,67},{4,68},{5,69},{6,70},{7,71},{32,96},{3... | collective-permute-start | bytes 786440 | tf_op jit(solution)/shard_map/ppermute | solution.py:38
  43.5 24.7 %collective-permute-start.21 = (bf16[2,128,512]{2,1,0:T(8,128)(2,1)}, bf16[2,128,512]{2,1,0:T(8,128)(2,1)}, u32[]{:S(2)}, u32[]{:S(2)}) collective-permute-start(bf16[2,128,512]{2,1,0:T(8,128)(2,1)} %get-tuple-element.57), channel_id=1, source_target_pairs={{0,192},{1,193},{2,194},{3,195},{4,196},{5,197},{6,198},{7,199},{8... | collective-permute-start | bytes 786440 | tf_op jit(solution)/shard_map/ppermute | solution.py:38
  58.8 8.0 %collective-permute-start.7 = (bf16[2,128,512]{2,1,0:T(8,128)(2,1)}, bf16[2,128,512]{2,1,0:T(8,128)(2,1)}, u32[]{:S(2)}, u32[]{:S(2)}) collective-permute-start(bf16[2,128,512]{2,1,0:T(8,128)(2,1)} %get-tuple-element.60), channel_id=1, source_target_pairs={{0,14},{1,15},{2,0},{3,1},{4,2},{5,3},{6,4},{7,5},{8,6},{9,7},{10,... | collective-permute-start | bytes 786440 | tf_op jit(solution)/shard_map/ppermute | solution.py:38
  58.8 8.0 %collective-permute-start.10 = (bf16[2,128,512]{2,1,0:T(8,128)(2,1)}, bf16[2,128,512]{2,1,0:T(8,128)(2,1)}, u32[]{:S(2)}, u32[]{:S(2)}) collective-permute-start(bf16[2,128,512]{2,1,0:T(8,128)(2,1)} %get-tuple-element.60), channel_id=1, source_target_pairs={{0,2},{1,3},{2,4},{3,5},{4,6},{5,7},{6,8},{7,9},{8,10},{9,11},{10,... | collective-permute-start | bytes 786440 | tf_op jit(solution)/shard_map/ppermute | solution.py:38
  61.0 7.2 %collective-permute-start.19 = (bf16[2,128,512]{2,1,0:T(8,128)(2,1)}, bf16[2,128,512]{2,1,0:T(8,128)(2,1)S(1)}, u32[]{:S(2)}, u32[]{:S(2)}) collective-permute-start(bf16[2,128,512]{2,1,0:T(8,128)(2,1)} %broadcast_select_fusion.3), channel_id=1, source_target_pairs={{0,64},{1,65},{2,66},{3,67},{4,68},{5,69},{6,70},{7,71},{24,88},{2... | collective-permute-start | bytes 786440 | tf_op jit(solution)/shard_map/ppermute | solution.py:38
  66.8 7.0 %collective-permute-start.8 = (bf16[2,128,512]{2,1,0:T(8,128)(2,1)}, bf16[2,128,512]{2,1,0:T(8,128)(2,1)S(1)}, u32[]{:S(2)}, u32[]{:S(2)}) collective-permute-start(bf16[2,128,512]{2,1,0:T(8,128)(2,1)} %collective-permute-done.7), channel_id=1, source_target_pairs={{0,14},{1,15},{2,0},{3,1},{4,2},{5,3},{6,4},{7,5},{8,6},{9,7},{10,... | collective-permute-start | bytes 786440 | tf_op jit(solution)/shard_map/ppermute | solution.py:38
  66.8 9.5 %collective-permute-start.11 = (bf16[2,128,512]{2,1,0:T(8,128)(2,1)}, bf16[2,128,512]{2,1,0:T(8,128)(2,1)S(1)}, u32[]{:S(2)}, u32[]{:S(2)}) collective-permute-start(bf16[2,128,512]{2,1,0:T(8,128)(2,1)} %collective-permute-done.10), channel_id=1, source_target_pairs={{0,2},{1,3},{2,4},{3,5},{4,6},{5,7},{6,8},{7,9},{8,10},{9,11},{10,... | collective-permute-start | bytes 786440 | tf_op jit(solution)/shard_map/ppermute | solution.py:38
  73.8 5.9 %collective-permute-start.9 = (bf16[2,128,512]{2,1,0:T(8,128)(2,1)S(1)}, bf16[2,128,512]{2,1,0:T(8,128)(2,1)S(1)}, u32[]{:S(2)}, u32[]{:S(2)}) collective-permute-start(bf16[2,128,512]{2,1,0:T(8,128)(2,1)S(1)} %collective-permute-done.8), channel_id=1, source_target_pairs={{0,14},{1,15},{2,0},{3,1},{4,2},{5,3},{6,4},{7,5},{8,6},{9,7},{10,... | collective-permute-start | bytes 786440 | tf_op jit(solution)/shard_map/ppermute | solution.py:38
  76.2 7.4 %collective-permute-start.12 = (bf16[2,128,512]{2,1,0:T(8,128)(2,1)S(1)}, bf16[2,128,512]{2,1,0:T(8,128)(2,1)S(1)}, u32[]{:S(2)}, u32[]{:S(2)}) collective-permute-start(bf16[2,128,512]{2,1,0:T(8,128)(2,1)S(1)} %collective-permute-done.11), channel_id=1, source_target_pairs={{0,2},{1,3},{2,4},{3,5},{4,6},{5,7},{6,8},{7,9},{8,10},{9,11},{10,... | collective-permute-start | bytes 786440 | tf_op jit(solution)/shard_map/ppermute | solution.py:38
  79.7 5.0 %collective-permute-start.14 = (bf16[128,512]{1,0:T(8,128)(2,1)S(1)}, bf16[128,512]{1,0:T(8,128)(2,1)S(1)}, u32[]{:S(2)}, u32[]{:S(2)}) collective-permute-start(bf16[128,512]{1,0:T(8,128)(2,1)S(1)} %slice_bitcast_fusion), channel_id=1, source_target_pairs={{0,14},{1,15},{2,0},{3,1},{4,2},{5,3},{6,4},{7,5},{8,6},{9,7},{10,... | collective-permute-start | bytes 393224 | tf_op jit(solution)/shard_map/ppermute | solution.py:38
  83.6 5.1 %collective-permute-start.13 = (bf16[128,512]{1,0:T(8,128)(2,1)S(1)}, bf16[128,512]{1,0:T(8,128)(2,1)S(1)}, u32[]{:S(2)}, u32[]{:S(2)}) collective-permute-start(bf16[128,512]{1,0:T(8,128)(2,1)S(1)} %slice_bitcast_fusion.1), channel_id=1, source_target_pairs={{0,2},{1,3},{2,4},{3,5},{4,6},{5,7},{6,8},{7,9},{8,10},{9,11},{10,... | collective-permute-start | bytes 393224 | tf_op jit(solution)/shard_map/ppermute | solution.py:38
  89.8 46.0 %collective-permute-start.15 = (bf16[8,2,128,512]{3,2,1,0:T(8,128)(2,1)S(1)}, bf16[8,2,128,512]{3,2,1,0:T(8,128)(2,1)S(1)}, u32[]{:S(2)}, u32[]{:S(2)}) collective-permute-start(bf16[8,2,128,512]{3,2,1,0:T(8,128)(2,1)S(1)} %bitcast_dynamic-update-slice_fusion.refs_1_), channel_id=1, source_target_pairs={{0,1},{1,0},{2,3},{3,2},{4,5},{5,4},{6,7},{7,6},{8,9},{9,8},{10,11... | collective-permute-start | bytes 6291464 | tf_op jit(solution)/shard_map/ppermute | solution.py:38
  93.9 13.7 %copy-start.1 = (f32[2048,512]{1,0:T(8,128)S(1)}, f32[2048,512]{1,0:T(8,128)}, u32[]{:S(2)}) copy-start(f32[2048,512]{1,0:T(8,128)} %block_ref.3) | copy-start | bytes 12582916
  93.9 13.5 %collective-permute-start.22 = (bf16[2,2,128,512]{3,2,1,0:T(8,128)(2,1)S(1)}, bf16[2,2,128,512]{3,2,1,0:T(8,128)(2,1)S(1)}, u32[]{:S(2)}, u32[]{:S(2)}) collective-permute-start(bf16[2,2,128,512]{3,2,1,0:T(8,128)(2,1)S(1)} %pad_maximum_fusion.1), channel_id=1, source_target_pairs={{0,32},{1,33},{2,34},{3,35},{4,36},{5,37},{6,38},{7,39},{8,40},{9,... | collective-permute-start | bytes 1572872 | tf_op jit(solution)/shard_map/ppermute | solution.py:38
  109.1 10.9 %collective-permute-start.27 = (bf16[1024,256]{1,0:T(8,128)(2,1)S(1)}, bf16[1024,256]{1,0:T(8,128)(2,1)S(1)}, u32[]{:S(2)}, u32[]{:S(2)}) collective-permute-start(bf16[1024,256]{1,0:T(8,128)(2,1)S(1)} %get-tuple-element.47.refs_0_), channel_id=1, source_target_pairs={{0,1},{1,2},{2,3},{3,4},{4,5},{5,6},{6,7},{7,8},{8,9},{9,10},{10,1... | collective-permute-start | bytes 1572872 | tf_op jit(solution)/shard_map/ppermute | solution.py:38
  111.1 10.5 %collective-permute-start.28 = (bf16[1024,256]{1,0:T(8,128)(2,1)S(1)}, bf16[1024,256]{1,0:T(8,128)(2,1)S(1)}, u32[]{:S(2)}, u32[]{:S(2)}) collective-permute-start(bf16[1024,256]{1,0:T(8,128)(2,1)S(1)} %get-tuple-element.48.refs_1_), channel_id=1, source_target_pairs={{1,0},{2,1},{3,2},{4,3},{5,4},{6,5},{7,6},{8,7},{9,8},{10,9},{11,1... | collective-permute-start | bytes 1572872 | tf_op jit(solution)/shard_map/ppermute | solution.py:38
  115.0 12.4 %collective-permute-start.23 = (bf16[1024,256]{1,0:T(8,128)(2,1)S(1)}, bf16[1024,256]{1,0:T(8,128)(2,1)S(1)}, u32[]{:S(2)}, u32[]{:S(2)}) collective-permute-start(bf16[1024,256]{1,0:T(8,128)(2,1)S(1)} %get-tuple-element.43.refs_0_), channel_id=1, source_target_pairs={{0,1},{1,2},{2,3},{3,4},{4,5},{5,6},{6,7},{7,8},{8,9},{9,10},{10,1... | collective-permute-start | bytes 1572872 | tf_op jit(solution)/shard_map/ppermute | solution.py:38
  118.2 10.5 %collective-permute-start.24 = (bf16[1024,256]{1,0:T(8,128)(2,1)S(1)}, bf16[1024,256]{1,0:T(8,128)(2,1)S(1)}, u32[]{:S(2)}, u32[]{:S(2)}) collective-permute-start(bf16[1024,256]{1,0:T(8,128)(2,1)S(1)} %get-tuple-element.44.refs_1_), channel_id=1, source_target_pairs={{1,0},{2,1},{3,2},{4,3},{5,4},{6,5},{7,6},{8,7},{9,8},{10,9},{11,1... | collective-permute-start | bytes 1572872 | tf_op jit(solution)/shard_map/ppermute | solution.py:38
  123.1 11.5 %collective-permute-start.29 = (bf16[1024,256]{1,0:T(8,128)(2,1)S(1)}, bf16[1024,256]{1,0:T(8,128)(2,1)S(1)}, u32[]{:S(2)}, u32[]{:S(2)}) collective-permute-start(bf16[1024,256]{1,0:T(8,128)(2,1)S(1)} %get-tuple-element.49.refs_3_), channel_id=1, source_target_pairs={{0,1},{1,2},{2,3},{3,4},{4,5},{5,6},{6,7},{7,8},{8,9},{9,10},{10,1... | collective-permute-start | bytes 1572872 | tf_op jit(solution)/shard_map/ppermute | solution.py:38
  125.3 10.5 %collective-permute-start.30 = (bf16[1024,256]{1,0:T(8,128)(2,1)S(1)}, bf16[1024,256]{1,0:T(8,128)(2,1)S(1)}, u32[]{:S(2)}, u32[]{:S(2)}) collective-permute-start(bf16[1024,256]{1,0:T(8,128)(2,1)S(1)} %get-tuple-element.50.refs_4_), channel_id=1, source_target_pairs={{1,0},{2,1},{3,2},{4,3},{5,4},{6,5},{7,6},{8,7},{9,8},{10,9},{11,1... | collective-permute-start | bytes 1572872 | tf_op jit(solution)/shard_map/ppermute | solution.py:38
  130.2 13.6 %collective-permute-start.25 = (bf16[1024,256]{1,0:T(8,128)(2,1)S(1)}, bf16[1024,256]{1,0:T(8,128)(2,1)S(1)}, u32[]{:S(2)}, u32[]{:S(2)}) collective-permute-start(bf16[1024,256]{1,0:T(8,128)(2,1)S(1)} %get-tuple-element.45.refs_3_), channel_id=1, source_target_pairs={{0,1},{1,2},{2,3},{3,4},{4,5},{5,6},{6,7},{7,8},{8,9},{9,10},{10,1... | collective-permute-start | bytes 1572872 | tf_op jit(solution)/shard_map/ppermute | solution.py:38
  132.4 11.4 %collective-permute-start.26 = (bf16[1024,256]{1,0:T(8,128)(2,1)S(1)}, bf16[1024,256]{1,0:T(8,128)(2,1)S(1)}, u32[]{:S(2)}, u32[]{:S(2)}) collective-permute-start(bf16[1024,256]{1,0:T(8,128)(2,1)S(1)} %get-tuple-element.46.refs_4_), channel_id=1, source_target_pairs={{1,0},{2,1},{3,2},{4,3},{5,4},{6,5},{7,6},{8,7},{9,8},{10,9},{11,1... | collective-permute-start | bytes 1572872 | tf_op jit(solution)/shard_map/ppermute | solution.py:38
  137.6 14.1 %collective-permute-start.31 = (bf16[256,512]{1,0:T(8,128)(2,1)S(1)}, bf16[256,512]{1,0:T(8,128)(2,1)S(1)}, u32[]{:S(2)}, u32[]{:S(2)}) collective-permute-start(bf16[256,512]{1,0:T(8,128)(2,1)S(1)} %get-tuple-element.52), channel_id=1, source_target_pairs={{0,32},{1,33},{2,34},{3,35},{4,36},{5,37},{6,38},{7,39},{8,40},{9,... | collective-permute-start | bytes 786440 | tf_op jit(solution)/shard_map/ppermute | solution.py:38
  139.7 22.7 %collective-permute-start.32 = (bf16[256,512]{1,0:T(8,128)(2,1)S(1)}, bf16[256,512]{1,0:T(8,128)(2,1)S(1)}, u32[]{:S(2)}, u32[]{:S(2)}) collective-permute-start(bf16[256,512]{1,0:T(8,128)(2,1)S(1)} %get-tuple-element.53), channel_id=1, source_target_pairs={{32,0},{33,1},{34,2},{35,3},{36,4},{37,5},{38,6},{39,7},{40,8},{41... | collective-permute-start | bytes 786440 | tf_op jit(solution)/shard_map/ppermute | solution.py:38
  165.1 10.3 %collective-permute-start.33 = (bf16[256,512]{1,0:T(8,128)(2,1)S(1)}, bf16[256,512]{1,0:T(8,128)(2,1)S(1)}, u32[]{:S(2)}, u32[]{:S(2)}) collective-permute-start(bf16[256,512]{1,0:T(8,128)(2,1)S(1)} %get-tuple-element.54), channel_id=1, source_target_pairs={{0,32},{1,33},{2,34},{3,35},{4,36},{5,37},{6,38},{7,39},{8,40},{9,... | collective-permute-start | bytes 786440 | tf_op jit(solution)/shard_map/ppermute | solution.py:38
  167.0 14.7 %collective-permute-start.34 = (bf16[256,512]{1,0:T(8,128)(2,1)S(1)}, bf16[256,512]{1,0:T(8,128)(2,1)S(1)}, u32[]{:S(2)}, u32[]{:S(2)}) collective-permute-start(bf16[256,512]{1,0:T(8,128)(2,1)S(1)} %get-tuple-element.55), channel_id=1, source_target_pairs={{32,0},{33,1},{34,2},{35,3},{36,4},{37,5},{38,6},{39,7},{40,8},{41... | collective-permute-start | bytes 786440 | tf_op jit(solution)/shard_map/ppermute | solution.py:38

commit v2 on v1

--- a/solution.py
+++ b/solution.py
@@ -103,8 +103,10 @@
 NEXT_DIAG = [(dev(k // 4, k), dev((k + 1) // 4, k + 1)) for k in range(COLS - 1)]
 PREV_DIAG = [(dev(k // 4, k), dev((k - 1) // 4, k - 1)) for k in range(1, COLS)]
 CROSS = [(dev(max(k - 1, 0) // 4, k + 1), dev(k // 4, k)) for k in range(COLS - 1)]
-COL_RIGHT = [(dev(r, c), dev(r, c + 1)) for r, c in GRID if c + 1 < COLS]
-COL_LEFT = [(dev(r, c), dev(r, c - 1)) for r, c in GRID if c > 0]
+COL_NEAR = CORE_SWAP
+COL_FAR = [
+    (dev(r, c), dev(r, c + 2 * (c % 2) - 1)) for r, c in GRID if 0 < c < COLS - 1
+]
 ROW_DOWN = [(dev(r, c), dev(r + 1, c)) for r, c in GRID if r + 1 < ROWS]
 ROW_UP = [(dev(r, c), dev(r - 1, c)) for r, c in GRID if r > 0]
 
@@ -278,26 +280,27 @@
 INNER = (1, 1)
 
 
-def store_halves(flags, product, right_ref, left_ref):
+def store_halves(flags, product, near_ref, far_ref):
     up = product[:, :H]
     low = product[:, H:]
-    first = flags[2] == 1
-    right_ref[...] = jnp.where(first, low, up)
-    left_ref[...] = jnp.where(first, up, low)
-
-
-def joined(flags, own_right, own_left, came_right, came_left):
-    up = jnp.where(flags[2] == 1, own_left[...], came_right[...])
-    low = jnp.where(flags[3] == 1, own_right[...], came_left[...])
-    return jnp.concatenate([up, low], 1)
-
-
-def half_specs(base, stride):
+    low_first = jnp.logical_or(flags[2] == 1, flags[8] == 1)
+    near_ref[...] = jnp.where(low_first, low, up)
+    far_ref[...] = jnp.where(low_first, up, low)
+
+
+def joined(flags, own_far, got_near, got_far):
+    at_end = jnp.logical_or(flags[2] == 1, flags[3] == 1)
+    far = jnp.where(at_end, own_far[...], got_far[...])
+    near = got_near[...]
+    odd = flags[8] == 1
+    return jnp.concatenate([jnp.where(odd, near, far), jnp.where(odd, far, near)], 1)
+
+
+def half_specs():
     return [
-        pl.BlockSpec((N, H), lambda i, f: ((base + stride * i) * f[3], 0)),
-        pl.BlockSpec((N, H), lambda i, f: ((base + stride * i) * f[2], 0)),
-        pl.BlockSpec((N, H), lambda i, f: (base + stride * i, 0)),
-        pl.BlockSpec((N, H), lambda i, f: (base + stride * i, 0)),
+        pl.BlockSpec((N, H), lambda i, f: (i * (f[2] + f[3]), 0)),
+        pl.BlockSpec((N, H), lambda i, f: (i, 0)),
+        pl.BlockSpec((N, H), lambda i, f: (i, 0)),
     ]
 
 
@@ -307,8 +310,8 @@
 
 
 def right_two_body(flags, *refs):
-    rot_ref, right_ref, left_ref = refs[4:]
-    product = mm(joined(flags, *refs[:4]), rot_ref[...].reshape(N, N)).astype(BF)
+    rot_ref, right_ref, left_ref = refs[3:]
+    product = mm(joined(flags, *refs[:3]), rot_ref[...].reshape(N, N)).astype(BF)
     store_halves(flags, product, right_ref, left_ref)
 
 
@@ -323,7 +326,7 @@
         (
             [pl.BlockSpec((N, N), lambda i, f: (base + stride * i, 0))]
             if first
-            else half_specs(0, 1)
+            else half_specs()
         )
         + [pl.BlockSpec((4, 1, Q, N), lambda i, f: (0, slot, 0, 0))],
         [out, out],
@@ -359,8 +362,8 @@
     edge = pairs == EDGE
     mine, theirs = refs[:2]
     if slot == 0:
-        block = joined(flags, *refs[2:6])
-        rest = refs[6:]
+        block = joined(flags, *refs[2:5])
+        rest = refs[5:]
     elif edge:
         block = with_ends(flags, step, *refs[2:5])
         rest = refs[5:]
@@ -418,7 +421,7 @@
     edge = pairs == EDGE
     pieces = pl.BlockSpec((8, 1, Q, N), lambda i, f: (0, slot, 0, 0))
     if slot == 0:
-        specs = half_specs(0, 1)
+        specs = half_specs()
     else:
         specs = [pl.BlockSpec((N, N), lambda i, f: (base + stride * i, 0))]
     specs = specs + [whole((H, N))] * len(ends)
@@ -479,7 +482,8 @@
 
 
 def exchange_columns(halves):
-    return (*halves, move(halves[0], COL_RIGHT), move(halves[1], COL_LEFT))
+    near, far = halves
+    return far, move(near, COL_NEAR), move(far, COL_FAR)
 
 
 def steps(factor):

time: 184 us -> 179 us (0.973)
  starting transfers between devices: 55.1 us -> 47.7 us
    ppermute x35, starting transfers between devices: 55.1 us -> 47.7 us  [move(): return lax.ppermute(value, ALL, pairs)]
where the time goes in v2:
time: 179 us; the launch traced here: 178 us
  waiting for transfers between devices  99.1 us (55%)
  starting transfers between devices  47.7 us (27%)
  Pallas kernels  19.6 us (11%)
  other arithmetic  5.71 us (3%)
  local copies, waits for them, and re-layouts  4.92 us (3%)
    ppermute x35, waiting for transfers between devices, move(): return lax.ppermute(value, ALL, pairs)  99.1 us
    ppermute x35, starting transfers between devices, move(): return lax.ppermute(value, ALL, pairs)  47.7 us
    pallas_call x12, Pallas kernels, call(): pl.pallas_call(body, grid_spec=pltpu.PrefetchScalarGridSpec(num_scalar_pr...  19.6 us
  transfers between devices with their start and end apart: 35, of which 16 were waited for; matrix products, arithmetic and copies ran while one was open for 4% of the time, Pallas kernels for 8%

profile of v2, /device:TPU:7, one launch (start us, length us, event | category | flops | bytes accessed | tf_op | source)
XLA Modules:
  0.0 177.9 jit_solution(5888903214844194877)
XLA Ops:
  0.7 2.2 %copy-done = f32[2048,512]{1,0:T(8,128)S(1)} copy-done((f32[2048,512]{1,0:T(8,128)S(1)}, f32[2048,512]{1,0:T(8,128)}, u32[]{:S(2)}) %copy-start) | copy-done | bytes 4194328
  2.9 1.5 cross_block.1
  5.1 1.3 solve_one.1
  7.7 1.4 collective-permute-start
  9.1 1.4 collective-permute-start.16
  11.7 1.0 select_bitcast_fusion.5
  14.3 1.3 collective-permute-start.20
  15.7 1.3 collective-permute-start.6
  17.0 25.0 %collective-permute-done.20 = bf16[2,128,512]{2,1,0:T(8,128)(2,1)S(1)} collective-permute-done((bf16[2,128,512]{2,1,0:T(8,128)(2,1)S(1)}, bf16[2,128,512]{2,1,0:T(8,128)(2,1)S(1)}, u32[]{:S(2)}, u32[]{:S(2)}) %collective-permute-start.20) | collective-permute-done | bytes 262176 | tf_op jit(solution)/shard_map/ppermute | solution.py:38
  43.5 1.9 %collective-permute-start.21 = (bf16[2,128,512]{2,1,0:T(8,128)(2,1)}, bf16[2,128,512]{2,1,0:T(8,128)(2,1)}, u32[]{:S(2)}, u32[]{:S(2)}) collective-permute-start(bf16[2,128,512]{2,1,0:T(8,128)(2,1)} %get-tuple-element.57), channel_id=1, source_target_pairs={{0,192},{1,193},{2,194},{3,195},{4,196},{5,197},{6,198},{7,199},{8... | collective-permute-start | bytes 786440 | tf_op jit(solution)/shard_map/ppermute | solution.py:38
  45.4 11.6 %collective-permute-done.6 = bf16[2,128,512]{2,1,0:T(8,128)(2,1)} collective-permute-done((bf16[2,128,512]{2,1,0:T(8,128)(2,1)S(1)}, bf16[2,128,512]{2,1,0:T(8,128)(2,1)}, u32[]{:S(2)}, u32[]{:S(2)}) %collective-permute-start.6) | collective-permute-done | bytes 262176 | tf_op jit(solution)/shard_map/ppermute | solution.py:38
  57.1 1.8 bitcast_dynamic-update-slice_fusion.6
  58.8 1.5 collective-permute-start.10
  61.7 5.1 %collective-permute-done.7 = bf16[2,128,512]{2,1,0:T(8,128)(2,1)} collective-permute-done((bf16[2,128,512]{2,1,0:T(8,128)(2,1)}, bf16[2,128,512]{2,1,0:T(8,128)(2,1)}, u32[]{:S(2)}, u32[]{:S(2)}) %collective-permute-start.7) | collective-permute-done | bytes 262176 | tf_op jit(solution)/shard_map/ppermute | solution.py:38
  66.8 1.5 collective-permute-start.11
  68.2 1.0 select_bitcast_fusion.1
  69.3 4.5 %collective-permute-done.8 = bf16[2,128,512]{2,1,0:T(8,128)(2,1)S(1)} collective-permute-done((bf16[2,128,512]{2,1,0:T(8,128)(2,1)}, bf16[2,128,512]{2,1,0:T(8,128)(2,1)S(1)}, u32[]{:S(2)}, u32[]{:S(2)}) %collective-permute-start.8) | collective-permute-done | bytes 262176 | tf_op jit(solution)/shard_map/ppermute | solution.py:38
  73.8 1.5 collective-permute-start.9
  76.5 3.2 %collective-permute-done.9 = bf16[2,128,512]{2,1,0:T(8,128)(2,1)S(1)} collective-permute-done((bf16[2,128,512]{2,1,0:T(8,128)(2,1)S(1)}, bf16[2,128,512]{2,1,0:T(8,128)(2,1)S(1)}, u32[]{:S(2)}, u32[]{:S(2)}) %collective-permute-start.9) | collective-permute-done | bytes 262176 | tf_op jit(solution)/shard_map/ppermute | solution.py:38
  79.7 3.1 %collective-permute-start.14 = (bf16[128,512]{1,0:T(8,128)(2,1)S(1)}, bf16[128,512]{1,0:T(8,128)(2,1)S(1)}, u32[]{:S(2)}, u32[]{:S(2)}) collective-permute-start(bf16[128,512]{1,0:T(8,128)(2,1)S(1)} %slice_bitcast_fusion), channel_id=1, source_target_pairs={{0,14},{1,15},{2,0},{3,1},{4,2},{5,3},{6,4},{7,5},{8,6},{9,7},{10,... | collective-permute-start | bytes 393224 | tf_op jit(solution)/shard_map/ppermute | solution.py:38
  84.7 4.0 %collective-permute-done.13 = bf16[128,512]{1,0:T(8,128)(2,1)S(1)} collective-permute-done((bf16[128,512]{1,0:T(8,128)(2,1)S(1)}, bf16[128,512]{1,0:T(8,128)(2,1)S(1)}, u32[]{:S(2)}, u32[]{:S(2)}) %collective-permute-start.13) | collective-permute-done | bytes 131104 | tf_op jit(solution)/shard_map/ppermute | solution.py:38
  88.8 1.0 bitcast_dynamic-update-slice_fusion.refs_1_
  89.8 4.0 %collective-permute-start.15 = (bf16[8,2,128,512]{3,2,1,0:T(8,128)(2,1)S(1)}, bf16[8,2,128,512]{3,2,1,0:T(8,128)(2,1)S(1)}, u32[]{:S(2)}, u32[]{:S(2)}) collective-permute-start(bf16[8,2,128,512]{3,2,1,0:T(8,128)(2,1)S(1)} %bitcast_dynamic-update-slice_fusion.refs_1_), channel_id=1, source_target_pairs={{0,1},{1,0},{2,3},{3,2},{4,5},{5,4},{6,7},{7,6},{8,9},{9,8},{10,11... | collective-permute-start | bytes 6291464 | tf_op jit(solution)/shard_map/ppermute | solution.py:38
  94.0 13.4 %collective-permute-done.22 = bf16[2,2,128,512]{3,2,1,0:T(8,128)(2,1)S(1)} collective-permute-done((bf16[2,2,128,512]{3,2,1,0:T(8,128)(2,1)S(1)}, bf16[2,2,128,512]{3,2,1,0:T(8,128)(2,1)S(1)}, u32[]{:S(2)}, u32[]{:S(2)}) %collective-permute-start.22) | collective-permute-done | bytes 524320 | tf_op jit(solution)/shard_map/ppermute | solution.py:38
  107.6 1.5 right.6
  110.1 1.9 %collective-permute-start.28 = (bf16[1024,256]{1,0:T(8,128)(2,1)S(1)}, bf16[1024,256]{1,0:T(8,128)(2,1)S(1)}, u32[]{:S(2)}, u32[]{:S(2)}) collective-permute-start(bf16[1024,256]{1,0:T(8,128)(2,1)S(1)} %get-tuple-element.47.refs_0_), channel_id=1, source_target_pairs={{1,2},{2,1},{3,4},{4,3},{5,6},{6,5},{7,8},{8,7},{9,10},{10,9},{11,... | collective-permute-start | bytes 1572872 | tf_op jit(solution)/shard_map/ppermute | solution.py:38
  112.0 1.5 right.4
  113.6 3.6 %collective-permute-start.24 = (bf16[1024,256]{1,0:T(8,128)(2,1)S(1)}, bf16[1024,256]{1,0:T(8,128)(2,1)S(1)}, u32[]{:S(2)}, u32[]{:S(2)}) collective-permute-start(bf16[1024,256]{1,0:T(8,128)(2,1)S(1)} %get-tuple-element.43.refs_0_), channel_id=1, source_target_pairs={{1,2},{2,1},{3,4},{4,3},{5,6},{6,5},{7,8},{8,7},{9,10},{10,9},{11,... | collective-permute-start | bytes 1572872 | tf_op jit(solution)/shard_map/ppermute | solution.py:38
  117.3 3.3 %collective-permute-done.28.refs_2_ = bf16[1024,256]{1,0:T(8,128)(2,1)S(1)} collective-permute-done((bf16[1024,256]{1,0:T(8,128)(2,1)S(1)}, bf16[1024,256]{1,0:T(8,128)(2,1)S(1)}, u32[]{:S(2)}, u32[]{:S(2)}) %collective-permute-start.28) | collective-permute-done | bytes 524320 | tf_op jit(solution)/shard_map/ppermute | solution.py:38
  120.6 1.5 right.7
  122.2 1.9 %collective-permute-start.30 = (bf16[1024,256]{1,0:T(8,128)(2,1)S(1)}, bf16[1024,256]{1,0:T(8,128)(2,1)S(1)}, u32[]{:S(2)}, u32[]{:S(2)}) collective-permute-start(bf16[1024,256]{1,0:T(8,128)(2,1)S(1)} %get-tuple-element.49.refs_3_), channel_id=1, source_target_pairs={{1,2},{2,1},{3,4},{4,3},{5,6},{6,5},{7,8},{8,7},{9,10},{10,9},{11,... | collective-permute-start | bytes 1572872 | tf_op jit(solution)/shard_map/ppermute | solution.py:38
  124.1 2.1 %collective-permute-done.24.refs_2_ = bf16[1024,256]{1,0:T(8,128)(2,1)S(1)} collective-permute-done((bf16[1024,256]{1,0:T(8,128)(2,1)S(1)}, bf16[1024,256]{1,0:T(8,128)(2,1)S(1)}, u32[]{:S(2)}, u32[]{:S(2)}) %collective-permute-start.24) | collective-permute-done | bytes 524320 | tf_op jit(solution)/shard_map/ppermute | solution.py:38
  126.2 1.5 right.5
  127.8 2.0 %collective-permute-start.26 = (bf16[1024,256]{1,0:T(8,128)(2,1)S(1)}, bf16[1024,256]{1,0:T(8,128)(2,1)S(1)}, u32[]{:S(2)}, u32[]{:S(2)}) collective-permute-start(bf16[1024,256]{1,0:T(8,128)(2,1)S(1)} %get-tuple-element.45.refs_3_), channel_id=1, source_target_pairs={{1,2},{2,1},{3,4},{4,3},{5,6},{6,5},{7,8},{8,7},{9,10},{10,9},{11,... | collective-permute-start | bytes 1572872 | tf_op jit(solution)/shard_map/ppermute | solution.py:38
  129.9 2.8 %collective-permute-done.30.refs_5_ = bf16[1024,256]{1,0:T(8,128)(2,1)S(1)} collective-permute-done((bf16[1024,256]{1,0:T(8,128)(2,1)S(1)}, bf16[1024,256]{1,0:T(8,128)(2,1)S(1)}, u32[]{:S(2)}, u32[]{:S(2)}) %collective-permute-start.30) | collective-permute-done | bytes 524320 | tf_op jit(solution)/shard_map/ppermute | solution.py:38
  132.7 1.8 left_edge.2
  134.5 1.9 %collective-permute-start.31 = (bf16[256,512]{1,0:T(8,128)(2,1)S(1)}, bf16[256,512]{1,0:T(8,128)(2,1)S(1)}, u32[]{:S(2)}, u32[]{:S(2)}) collective-permute-start(bf16[256,512]{1,0:T(8,128)(2,1)S(1)} %get-tuple-element.52), channel_id=1, source_target_pairs={{0,32},{1,33},{2,34},{3,35},{4,36},{5,37},{6,38},{7,39},{8,40},{9,... | collective-permute-start | bytes 786440 | tf_op jit(solution)/shard_map/ppermute | solution.py:38
  136.4 4.3 %collective-permute-start.32 = (bf16[256,512]{1,0:T(8,128)(2,1)S(1)}, bf16[256,512]{1,0:T(8,128)(2,1)S(1)}, u32[]{:S(2)}, u32[]{:S(2)}) collective-permute-start(bf16[256,512]{1,0:T(8,128)(2,1)S(1)} %get-tuple-element.53), channel_id=1, source_target_pairs={{32,0},{33,1},{34,2},{35,3},{36,4},{37,5},{38,6},{39,7},{40,8},{41... | collective-permute-start | bytes 786440 | tf_op jit(solution)/shard_map/ppermute | solution.py:38
  140.7 1.7 left_inner.2.refs_3_
  142.4 8.1 %collective-permute-done.31.refs_4_ = bf16[256,512]{1,0:T(8,128)(2,1)S(1)} collective-permute-done((bf16[256,512]{1,0:T(8,128)(2,1)S(1)}, bf16[256,512]{1,0:T(8,128)(2,1)S(1)}, u32[]{:S(2)}, u32[]{:S(2)}) %collective-permute-start.31) | collective-permute-done | bytes 262176 | tf_op jit(solution)/shard_map/ppermute | solution.py:38
  150.5 6.3 %collective-permute-done.32.refs_5_ = bf16[256,512]{1,0:T(8,128)(2,1)S(1)} collective-permute-done((bf16[256,512]{1,0:T(8,128)(2,1)S(1)}, bf16[256,512]{1,0:T(8,128)(2,1)S(1)}, u32[]{:S(2)}, u32[]{:S(2)}) %collective-permute-start.32) | collective-permute-done | bytes 262176 | tf_op jit(solution)/shard_map/ppermute | solution.py:38
  156.8 2.7 %left_edge.3 = (f32[2048,512]{1,0:T(8,128)}, bf16[256,512]{1,0:T(8,128)(2,1)S(1)}, bf16[256,512]{1,0:T(8,128)(2,1)S(1)}) custom-call(s32[16]{0:T(128)S(1)} %dynamic-slice_bitcast_fusion.flags.refs_0_, bf16[8,2,128,512]{3,2,1,0:T(8,128)(2,1)S(1)} %bitcast_dynamic-update-slice_fusion.refs_1_, bf16[8,2,128,512]{3,2,1,0:T(8,128)(2,1)S(1)} %collective-permute-done.15.refs_2_, ...), custom_call_target="tpu_custom_call" | custom-call | tf_op jit(solution)/shard_map/left_edge/pallas_call | solution.py:201
  159.5 1.9 %collective-permute-start.33 = (bf16[256,512]{1,0:T(8,128)(2,1)S(1)}, bf16[256,512]{1,0:T(8,128)(2,1)S(1)}, u32[]{:S(2)}, u32[]{:S(2)}) collective-permute-start(bf16[256,512]{1,0:T(8,128)(2,1)S(1)} %get-tuple-element.54), channel_id=1, source_target_pairs={{0,32},{1,33},{2,34},{3,35},{4,36},{5,37},{6,38},{7,39},{8,40},{9,... | collective-permute-start | bytes 786440 | tf_op jit(solution)/shard_map/ppermute | solution.py:38
  161.4 4.3 %collective-permute-start.34 = (bf16[256,512]{1,0:T(8,128)(2,1)S(1)}, bf16[256,512]{1,0:T(8,128)(2,1)S(1)}, u32[]{:S(2)}, u32[]{:S(2)}) collective-permute-start(bf16[256,512]{1,0:T(8,128)(2,1)S(1)} %get-tuple-element.55), channel_id=1, source_target_pairs={{32,0},{33,1},{34,2},{35,3},{36,4},{37,5},{38,6},{39,7},{40,8},{41... | collective-permute-start | bytes 786440 | tf_op jit(solution)/shard_map/ppermute | solution.py:38
  165.7 2.6 %left_inner.3.main_ref = f32[2048,512]{1,0:T(8,128)} custom-call(s32[16]{0:T(128)S(1)} %dynamic-slice_bitcast_fusion.flags.refs_0_, bf16[8,2,128,512]{3,2,1,0:T(8,128)(2,1)S(1)} %bitcast_dynamic-update-slice_fusion.refs_1_, bf16[8,2,128,512]{3,2,1,0:T(8,128)(2,1)S(1)} %collective-permute-done.15.refs_2_, ...), custom_call_target="tpu_custom_call", output_to_operand_aliasing={{}: (4, {})} | custom-call | tf_op jit(solution)/shard_map/left_inner/pallas_call | solution.py:201
  168.3 1.5 collective-permute-done.33.above_ref
  169.8 6.3 %collective-permute-done.34.below_ref = bf16[256,512]{1,0:T(8,128)(2,1)S(1)} collective-permute-done((bf16[256,512]{1,0:T(8,128)(2,1)S(1)}, bf16[256,512]{1,0:T(8,128)(2,1)S(1)}, u32[]{:S(2)}, u32[]{:S(2)}) %collective-permute-start.34) | collective-permute-done | bytes 262176 | tf_op jit(solution)/shard_map/ppermute | solution.py:38
  176.2 1.6 settle.1
  (62 shorter events, 13.2 us)
Async XLA Ops:
  0.7 2.2 %copy-start = (f32[2048,512]{1,0:T(8,128)S(1)}, f32[2048,512]{1,0:T(8,128)}, u32[]{:S(2)}) copy-start(f32[2048,512]{1,0:T(8,128)} %block_ref.3) | copy-start | bytes 12582916
  4.4 6.1 %collective-permute-start.3 = (bf16[512,512]{1,0:T(8,128)(2,1)}, bf16[512,512]{1,0:T(8,128)(2,1)S(1)}, u32[]{:S(2)}, u32[]{:S(2)}) collective-permute-start(bf16[512,512]{1,0:T(8,128)(2,1)} %get-tuple-element.35), channel_id=1, source_target_pairs={{1,0},{2,1},{3,2},{4,3},{5,36},{38,37},{39,38},{40,39},{41,72},{74... | collective-permute-start | bytes 1572872 | tf_op jit(solution)/shard_map/ppermute | solution.py:38
  6.3 4.2 %collective-permute-start.1 = (bf16[768,256]{1,0:T(8,128)(2,1)S(1)}, bf16[768,256]{1,0:T(8,128)(2,1)S(1)}, u32[]{:S(2)}, u32[]{:S(2)}) collective-permute-start(bf16[768,256]{1,0:T(8,128)(2,1)S(1)} %get-tuple-element.33.own_right), channel_id=1, source_target_pairs={{0,1},{1,2},{2,3},{3,36},{36,37},{37,38},{38,39},{39,72},{72,73},{... | collective-permute-start | bytes 1179656 | tf_op jit(solution)/shard_map/ppermute | solution.py:38
  7.0 3.5 %collective-permute-start.2 = (bf16[768,256]{1,0:T(8,128)(2,1)S(1)}, bf16[768,256]{1,0:T(8,128)(2,1)S(1)}, u32[]{:S(2)}, u32[]{:S(2)}) collective-permute-start(bf16[768,256]{1,0:T(8,128)(2,1)S(1)} %get-tuple-element.34.own_left), channel_id=1, source_target_pairs={{1,0},{2,1},{3,2},{36,3},{37,36},{38,37},{39,38},{72,39},{73,72},{... | collective-permute-start | bytes 1179656 | tf_op jit(solution)/shard_map/ppermute | solution.py:38
  7.7 4.0 %collective-permute-start = (bf16[2,128,512]{2,1,0:T(8,128)(2,1)}, bf16[2,128,512]{2,1,0:T(8,128)(2,1)}, u32[]{:S(2)}, u32[]{:S(2)}) collective-permute-start(bf16[2,128,512]{2,1,0:T(8,128)(2,1)} %get-tuple-element.32), channel_id=1, source_target_pairs={{0,12},{1,13},{36,32},{37,33},{72,68},{73,69},{108,104},{109,105},... | collective-permute-start | bytes 786440 | tf_op jit(solution)/shard_map/ppermute | solution.py:38
  9.1 3.6 %collective-permute-start.16 = (bf16[2,128,512]{2,1,0:T(8,128)(2,1)S(1)}, bf16[2,128,512]{2,1,0:T(8,128)(2,1)}, u32[]{:S(2)}, u32[]{:S(2)}) collective-permute-start(bf16[2,128,512]{2,1,0:T(8,128)(2,1)S(1)} %get-tuple-element.40), channel_id=1, source_target_pairs={{0,32},{1,33},{2,34},{3,35},{36,4},{37,5},{38,6},{39,7},{72,104},{... | collective-permute-start | bytes 786440 | tf_op jit(solution)/shard_map/ppermute | solution.py:38
  11.1 2.4 %collective-permute-start.4 = (bf16[2,128,512]{2,1,0:T(8,128)(2,1)S(1)}, bf16[2,128,512]{2,1,0:T(8,128)(2,1)S(1)}, u32[]{:S(2)}, u32[]{:S(2)}) collective-permute-start(bf16[2,128,512]{2,1,0:T(8,128)(2,1)S(1)} %get-tuple-element.38), channel_id=1, source_target_pairs={{0,12},{1,13},{36,32},{37,33},{72,68},{73,69},{108,104},{109,105},... | collective-permute-start | bytes 786440 | tf_op jit(solution)/shard_map/ppermute | solution.py:38
  12.8 1.5 collective-permute-start.17
  13.6 2.1 %collective-permute-start.5 = (bf16[2,128,512]{2,1,0:T(8,128)(2,1)S(1)}, bf16[2,128,512]{2,1,0:T(8,128)(2,1)S(1)}, u32[]{:S(2)}, u32[]{:S(2)}) collective-permute-start(bf16[2,128,512]{2,1,0:T(8,128)(2,1)S(1)} %fusion.3), channel_id=1, source_target_pairs={{0,14},{1,15},{12,10},{13,11},{32,46},{33,47},{36,34},{37,35},{68,... | collective-permute-start | bytes 786440 | tf_op jit(solution)/shard_map/ppermute | solution.py:38
  14.3 27.7 %collective-permute-start.20 = (bf16[2,128,512]{2,1,0:T(8,128)(2,1)S(1)}, bf16[2,128,512]{2,1,0:T(8,128)(2,1)S(1)}, u32[]{:S(2)}, u32[]{:S(2)}) collective-permute-start(bf16[2,128,512]{2,1,0:T(8,128)(2,1)S(1)} %fusion.4), channel_id=1, source_target_pairs={{0,192},{1,193},{2,194},{3,195},{4,196},{5,197},{6,198},{7,199},{3... | collective-permute-start | bytes 786440 | tf_op jit(solution)/shard_map/ppermute | solution.py:38
  15.7 41.3 %collective-permute-start.6 = (bf16[2,128,512]{2,1,0:T(8,128)(2,1)S(1)}, bf16[2,128,512]{2,1,0:T(8,128)(2,1)}, u32[]{:S(2)}, u32[]{:S(2)}) collective-permute-start(bf16[2,128,512]{2,1,0:T(8,128)(2,1)S(1)} %fusion.6), channel_id=1, source_target_pairs={{0,16},{1,17},{2,18},{3,19},{4,20},{5,21},{6,22},{7,23},{8,24},{9,... | collective-permute-start | bytes 786440 | tf_op jit(solution)/shard_map/ppermute | solution.py:38
  42.8 17.5 %collective-permute-start.18 = (bf16[2,128,512]{2,1,0:T(8,128)(2,1)S(1)}, bf16[2,128,512]{2,1,0:T(8,128)(2,1)S(1)}, u32[]{:S(2)}, u32[]{:S(2)}) collective-permute-start(bf16[2,128,512]{2,1,0:T(8,128)(2,1)S(1)} %get-tuple-element.58), channel_id=1, source_target_pairs={{0,64},{1,65},{2,66},{3,67},{4,68},{5,69},{6,70},{7,71},{32,96},{3... | collective-permute-start | bytes 786440 | tf_op jit(solution)/shard_map/ppermute | solution.py:38
  43.5 24.7 %collective-permute-start.21 = (bf16[2,128,512]{2,1,0:T(8,128)(2,1)}, bf16[2,128,512]{2,1,0:T(8,128)(2,1)}, u32[]{:S(2)}, u32[]{:S(2)}) collective-permute-start(bf16[2,128,512]{2,1,0:T(8,128)(2,1)} %get-tuple-element.57), channel_id=1, source_target_pairs={{0,192},{1,193},{2,194},{3,195},{4,196},{5,197},{6,198},{7,199},{8... | collective-permute-start | bytes 786440 | tf_op jit(solution)/shard_map/ppermute | solution.py:38
  58.8 8.0 %collective-permute-start.7 = (bf16[2,128,512]{2,1,0:T(8,128)(2,1)}, bf16[2,128,512]{2,1,0:T(8,128)(2,1)}, u32[]{:S(2)}, u32[]{:S(2)}) collective-permute-start(bf16[2,128,512]{2,1,0:T(8,128)(2,1)} %get-tuple-element.60), channel_id=1, source_target_pairs={{0,14},{1,15},{2,0},{3,1},{4,2},{5,3},{6,4},{7,5},{8,6},{9,7},{10,... | collective-permute-start | bytes 786440 | tf_op jit(solution)/shard_map/ppermute | solution.py:38
  58.8 8.0 %collective-permute-start.10 = (bf16[2,128,512]{2,1,0:T(8,128)(2,1)}, bf16[2,128,512]{2,1,0:T(8,128)(2,1)}, u32[]{:S(2)}, u32[]{:S(2)}) collective-permute-start(bf16[2,128,512]{2,1,0:T(8,128)(2,1)} %get-tuple-element.60), channel_id=1, source_target_pairs={{0,2},{1,3},{2,4},{3,5},{4,6},{5,7},{6,8},{7,9},{8,10},{9,11},{10,... | collective-permute-start | bytes 786440 | tf_op jit(solution)/shard_map/ppermute | solution.py:38
  61.0 7.2 %collective-permute-start.19 = (bf16[2,128,512]{2,1,0:T(8,128)(2,1)}, bf16[2,128,512]{2,1,0:T(8,128)(2,1)S(1)}, u32[]{:S(2)}, u32[]{:S(2)}) collective-permute-start(bf16[2,128,512]{2,1,0:T(8,128)(2,1)} %broadcast_select_fusion.3), channel_id=1, source_target_pairs={{0,64},{1,65},{2,66},{3,67},{4,68},{5,69},{6,70},{7,71},{24,88},{2... | collective-permute-start | bytes 786440 | tf_op jit(solution)/shard_map/ppermute | solution.py:38
  66.8 7.0 %collective-permute-start.8 = (bf16[2,128,512]{2,1,0:T(8,128)(2,1)}, bf16[2,128,512]{2,1,0:T(8,128)(2,1)S(1)}, u32[]{:S(2)}, u32[]{:S(2)}) collective-permute-start(bf16[2,128,512]{2,1,0:T(8,128)(2,1)} %collective-permute-done.7), channel_id=1, source_target_pairs={{0,14},{1,15},{2,0},{3,1},{4,2},{5,3},{6,4},{7,5},{8,6},{9,7},{10,... | collective-permute-start | bytes 786440 | tf_op jit(solution)/shard_map/ppermute | solution.py:38
  66.8 9.5 %collective-permute-start.11 = (bf16[2,128,512]{2,1,0:T(8,128)(2,1)}, bf16[2,128,512]{2,1,0:T(8,128)(2,1)S(1)}, u32[]{:S(2)}, u32[]{:S(2)}) collective-permute-start(bf16[2,128,512]{2,1,0:T(8,128)(2,1)} %collective-permute-done.10), channel_id=1, source_target_pairs={{0,2},{1,3},{2,4},{3,5},{4,6},{5,7},{6,8},{7,9},{8,10},{9,11},{10,... | collective-permute-start | bytes 786440 | tf_op jit(solution)/shard_map/ppermute | solution.py:38
  73.8 5.9 %collective-permute-start.9 = (bf16[2,128,512]{2,1,0:T(8,128)(2,1)S(1)}, bf16[2,128,512]{2,1,0:T(8,128)(2,1)S(1)}, u32[]{:S(2)}, u32[]{:S(2)}) collective-permute-start(bf16[2,128,512]{2,1,0:T(8,128)(2,1)S(1)} %collective-permute-done.8), channel_id=1, source_target_pairs={{0,14},{1,15},{2,0},{3,1},{4,2},{5,3},{6,4},{7,5},{8,6},{9,7},{10,... | collective-permute-start | bytes 786440 | tf_op jit(solution)/shard_map/ppermute | solution.py:38
  76.2 7.4 %collective-permute-start.12 = (bf16[2,128,512]{2,1,0:T(8,128)(2,1)S(1)}, bf16[2,128,512]{2,1,0:T(8,128)(2,1)S(1)}, u32[]{:S(2)}, u32[]{:S(2)}) collective-permute-start(bf16[2,128,512]{2,1,0:T(8,128)(2,1)S(1)} %collective-permute-done.11), channel_id=1, source_target_pairs={{0,2},{1,3},{2,4},{3,5},{4,6},{5,7},{6,8},{7,9},{8,10},{9,11},{10,... | collective-permute-start | bytes 786440 | tf_op jit(solution)/shard_map/ppermute | solution.py:38
  79.7 5.0 %collective-permute-start.14 = (bf16[128,512]{1,0:T(8,128)(2,1)S(1)}, bf16[128,512]{1,0:T(8,128)(2,1)S(1)}, u32[]{:S(2)}, u32[]{:S(2)}) collective-permute-start(bf16[128,512]{1,0:T(8,128)(2,1)S(1)} %slice_bitcast_fusion), channel_id=1, source_target_pairs={{0,14},{1,15},{2,0},{3,1},{4,2},{5,3},{6,4},{7,5},{8,6},{9,7},{10,... | collective-permute-start | bytes 393224 | tf_op jit(solution)/shard_map/ppermute | solution.py:38
  83.6 5.1 %collective-permute-start.13 = (bf16[128,512]{1,0:T(8,128)(2,1)S(1)}, bf16[128,512]{1,0:T(8,128)(2,1)S(1)}, u32[]{:S(2)}, u32[]{:S(2)}) collective-permute-start(bf16[128,512]{1,0:T(8,128)(2,1)S(1)} %slice_bitcast_fusion.1), channel_id=1, source_target_pairs={{0,2},{1,3},{2,4},{3,5},{4,6},{5,7},{6,8},{7,9},{8,10},{9,11},{10,... | collective-permute-start | bytes 393224 | tf_op jit(solution)/shard_map/ppermute | solution.py:38
  89.8 42.9 %collective-permute-start.15 = (bf16[8,2,128,512]{3,2,1,0:T(8,128)(2,1)S(1)}, bf16[8,2,128,512]{3,2,1,0:T(8,128)(2,1)S(1)}, u32[]{:S(2)}, u32[]{:S(2)}) collective-permute-start(bf16[8,2,128,512]{3,2,1,0:T(8,128)(2,1)S(1)} %bitcast_dynamic-update-slice_fusion.refs_1_), channel_id=1, source_target_pairs={{0,1},{1,0},{2,3},{3,2},{4,5},{5,4},{6,7},{7,6},{8,9},{9,8},{10,11... | collective-permute-start | bytes 6291464 | tf_op jit(solution)/shard_map/ppermute | solution.py:38
  93.9 13.7 %copy-start.1 = (f32[2048,512]{1,0:T(8,128)S(1)}, f32[2048,512]{1,0:T(8,128)}, u32[]{:S(2)}) copy-start(f32[2048,512]{1,0:T(8,128)} %block_ref.3) | copy-start | bytes 12582916
  93.9 13.5 %collective-permute-start.22 = (bf16[2,2,128,512]{3,2,1,0:T(8,128)(2,1)S(1)}, bf16[2,2,128,512]{3,2,1,0:T(8,128)(2,1)S(1)}, u32[]{:S(2)}, u32[]{:S(2)}) collective-permute-start(bf16[2,2,128,512]{3,2,1,0:T(8,128)(2,1)S(1)} %pad_maximum_fusion.1), channel_id=1, source_target_pairs={{0,32},{1,33},{2,34},{3,35},{4,36},{5,37},{6,38},{7,39},{8,40},{9,... | collective-permute-start | bytes 1572872 | tf_op jit(solution)/shard_map/ppermute | solution.py:38
  109.1 8.1 %collective-permute-start.27 = (bf16[1024,256]{1,0:T(8,128)(2,1)S(1)}, bf16[1024,256]{1,0:T(8,128)(2,1)S(1)}, u32[]{:S(2)}, u32[]{:S(2)}) collective-permute-start(bf16[1024,256]{1,0:T(8,128)(2,1)S(1)} %get-tuple-element.48), channel_id=1, source_target_pairs={{0,1},{1,0},{2,3},{3,2},{4,5},{5,4},{6,7},{7,6},{8,9},{9,8},{10,11... | collective-permute-start | bytes 1572872 | tf_op jit(solution)/shard_map/ppermute | solution.py:38
  110.1 10.5 %collective-permute-start.28 = (bf16[1024,256]{1,0:T(8,128)(2,1)S(1)}, bf16[1024,256]{1,0:T(8,128)(2,1)S(1)}, u32[]{:S(2)}, u32[]{:S(2)}) collective-permute-start(bf16[1024,256]{1,0:T(8,128)(2,1)S(1)} %get-tuple-element.47.refs_0_), channel_id=1, source_target_pairs={{1,2},{2,1},{3,4},{4,3},{5,6},{6,5},{7,8},{8,7},{9,10},{10,9},{11,... | collective-permute-start | bytes 1572872 | tf_op jit(solution)/shard_map/ppermute | solution.py:38
  113.5 10.6 %collective-permute-start.23 = (bf16[1024,256]{1,0:T(8,128)(2,1)S(1)}, bf16[1024,256]{1,0:T(8,128)(2,1)S(1)}, u32[]{:S(2)}, u32[]{:S(2)}) collective-permute-start(bf16[1024,256]{1,0:T(8,128)(2,1)S(1)} %get-tuple-element.44), channel_id=1, source_target_pairs={{0,1},{1,0},{2,3},{3,2},{4,5},{5,4},{6,7},{7,6},{8,9},{9,8},{10,11... | collective-permute-start | bytes 1572872 | tf_op jit(solution)/shard_map/ppermute | solution.py:38
  113.6 12.6 %collective-permute-start.24 = (bf16[1024,256]{1,0:T(8,128)(2,1)S(1)}, bf16[1024,256]{1,0:T(8,128)(2,1)S(1)}, u32[]{:S(2)}, u32[]{:S(2)}) collective-permute-start(bf16[1024,256]{1,0:T(8,128)(2,1)S(1)} %get-tuple-element.43.refs_0_), channel_id=1, source_target_pairs={{1,2},{2,1},{3,4},{4,3},{5,6},{6,5},{7,8},{8,7},{9,10},{10,9},{11,... | collective-permute-start | bytes 1572872 | tf_op jit(solution)/shard_map/ppermute | solution.py:38
  122.1 7.8 %collective-permute-start.29 = (bf16[1024,256]{1,0:T(8,128)(2,1)S(1)}, bf16[1024,256]{1,0:T(8,128)(2,1)S(1)}, u32[]{:S(2)}, u32[]{:S(2)}) collective-permute-start(bf16[1024,256]{1,0:T(8,128)(2,1)S(1)} %get-tuple-element.50), channel_id=1, source_target_pairs={{0,1},{1,0},{2,3},{3,2},{4,5},{5,4},{6,7},{7,6},{8,9},{9,8},{10,11... | collective-permute-start | bytes 1572872 | tf_op jit(solution)/shard_map/ppermute | solution.py:38
  122.2 10.5 %collective-permute-start.30 = (bf16[1024,256]{1,0:T(8,128)(2,1)S(1)}, bf16[1024,256]{1,0:T(8,128)(2,1)S(1)}, u32[]{:S(2)}, u32[]{:S(2)}) collective-permute-start(bf16[1024,256]{1,0:T(8,128)(2,1)S(1)} %get-tuple-element.49.refs_3_), channel_id=1, source_target_pairs={{1,2},{2,1},{3,4},{4,3},{5,6},{6,5},{7,8},{8,7},{9,10},{10,9},{11,... | collective-permute-start | bytes 1572872 | tf_op jit(solution)/shard_map/ppermute | solution.py:38
  127.7 13.0 %collective-permute-start.25 = (bf16[1024,256]{1,0:T(8,128)(2,1)S(1)}, bf16[1024,256]{1,0:T(8,128)(2,1)S(1)}, u32[]{:S(2)}, u32[]{:S(2)}) collective-permute-start(bf16[1024,256]{1,0:T(8,128)(2,1)S(1)} %get-tuple-element.46), channel_id=1, source_target_pairs={{0,1},{1,0},{2,3},{3,2},{4,5},{5,4},{6,7},{7,6},{8,9},{9,8},{10,11... | collective-permute-start | bytes 1572872 | tf_op jit(solution)/shard_map/ppermute | solution.py:38
  127.8 12.9 %collective-permute-start.26 = (bf16[1024,256]{1,0:T(8,128)(2,1)S(1)}, bf16[1024,256]{1,0:T(8,128)(2,1)S(1)}, u32[]{:S(2)}, u32[]{:S(2)}) collective-permute-start(bf16[1024,256]{1,0:T(8,128)(2,1)S(1)} %get-tuple-element.45.refs_3_), channel_id=1, source_target_pairs={{1,2},{2,1},{3,4},{4,3},{5,6},{6,5},{7,8},{8,7},{9,10},{10,9},{11,... | collective-permute-start | bytes 1572872 | tf_op jit(solution)/shard_map/ppermute | solution.py:38
  134.5 16.0 %collective-permute-start.31 = (bf16[256,512]{1,0:T(8,128)(2,1)S(1)}, bf16[256,512]{1,0:T(8,128)(2,1)S(1)}, u32[]{:S(2)}, u32[]{:S(2)}) collective-permute-start(bf16[256,512]{1,0:T(8,128)(2,1)S(1)} %get-tuple-element.52), channel_id=1, source_target_pairs={{0,32},{1,33},{2,34},{3,35},{4,36},{5,37},{6,38},{7,39},{8,40},{9,... | collective-permute-start | bytes 786440 | tf_op jit(solution)/shard_map/ppermute | solution.py:38
  136.4 20.4 %collective-permute-start.32 = (bf16[256,512]{1,0:T(8,128)(2,1)S(1)}, bf16[256,512]{1,0:T(8,128)(2,1)S(1)}, u32[]{:S(2)}, u32[]{:S(2)}) collective-permute-start(bf16[256,512]{1,0:T(8,128)(2,1)S(1)} %get-tuple-element.53), channel_id=1, source_target_pairs={{32,0},{33,1},{34,2},{35,3},{36,4},{37,5},{38,6},{39,7},{40,8},{41... | collective-permute-start | bytes 786440 | tf_op jit(solution)/shard_map/ppermute | solution.py:38
  159.5 10.3 %collective-permute-start.33 = (bf16[256,512]{1,0:T(8,128)(2,1)S(1)}, bf16[256,512]{1,0:T(8,128)(2,1)S(1)}, u32[]{:S(2)}, u32[]{:S(2)}) collective-permute-start(bf16[256,512]{1,0:T(8,128)(2,1)S(1)} %get-tuple-element.54), channel_id=1, source_target_pairs={{0,32},{1,33},{2,34},{3,35},{4,36},{5,37},{6,38},{7,39},{8,40},{9,... | collective-permute-start | bytes 786440 | tf_op jit(solution)/shard_map/ppermute | solution.py:38
  161.4 14.7 %collective-permute-start.34 = (bf16[256,512]{1,0:T(8,128)(2,1)S(1)}, bf16[256,512]{1,0:T(8,128)(2,1)S(1)}, u32[]{:S(2)}, u32[]{:S(2)}) collective-permute-start(bf16[256,512]{1,0:T(8,128)(2,1)S(1)} %get-tuple-element.55), channel_id=1, source_target_pairs={{32,0},{33,1},{34,2},{35,3},{36,4},{37,5},{38,6},{39,7},{40,8},{41... | collective-permute-start | bytes 786440 | tf_op jit(solution)/shard_map/ppermute | solution.py:38
